TPU v7x, 32 devices: a whole 2x2x4 slice. The times are simulated.
32 devices in a mesh: outer: 4 (over y, core), dev: 8 (over z, x).
Axes of the slice: x: 2, y: 2, z: 4, core: 2. Of those that a mesh axis runs over, the one named last changes fastest.
Arguments:
- gradients: bfloat16 [4, 8, 128, 20480], P('outer', 'dev'), may hold values from -6 to 6
- momentum: float32 [4, 128, 20480], P('outer', None, 'dev'), may hold values from -4 to 4
- chosen: int32 [4, 2, 320, 32], P(None, None, 'dev'), may hold values from 0 to 4095, as said below
Outputs:
- momentum_out: float32 [4, 128, 20480], P('outer', None, 'dev')
- update: float32 [128, 20480], P(None, 'dev')
Inputs may be any that keep to these rules, and one draw needn't show every extreme that they name: `chosen`: within each block the 32 positions are distinct; an entry i stands for row i // 64 and column i % 64 of the block's table.
All inputs are finite; a program needn't handle non-finite values.
Results may differ from a plain program's by a relative error of at most 0.0003.
Values sent between devices are 32-bit elements; how exact they have to be, the bound alone decides.
No kernel may reach another device: no remote copies, remote signals or barrier semaphores. Data moves between devices by JAX's collectives and lax.ppermute only.
A program may use at most 128 MiB of HBM per device.

v0:
```python
import jax
import jax.numpy as jnp
from jax import lax
from jax.sharding import PartitionSpec as P

GROUP = 64


decay_rate = 0.999
tiny_eps = 1e-06


def cosine_basis(size):
    freq = jnp.arange(size, dtype=jnp.float32)[:, None]
    place = jnp.arange(size, dtype=jnp.float32)[None, :]
    weight = jnp.where(
        freq == 0, jnp.sqrt(jnp.float32(1.0 / size)), jnp.sqrt(jnp.float32(2.0 / size))
    )
    return weight * jnp.cos(jnp.pi * (2.0 * place + 1.0) * freq / (2.0 * size))


def to_spectrum(spatial, basis):
    side = basis.shape[0]
    row_all, col_all = spatial.shape
    blocks = spatial.reshape(row_all // side, side, col_all // side, side)
    out = jnp.einsum("ij,rjsk,lk->sril", basis, blocks, basis, precision=lax.Precision.HIGHEST)
    return out.reshape(col_all // side, row_all // side, side * side)


def from_spectrum(spectrum, basis):
    side = basis.shape[0]
    col_blocks, row_blocks = (spectrum.shape[0], spectrum.shape[1])
    blocks = spectrum.reshape(col_blocks, row_blocks, side, side)
    out = jnp.einsum("ij,sril,lk->rjsk", basis, blocks, basis, precision=lax.Precision.HIGHEST)
    return out.reshape(row_blocks * side, col_blocks * side)


def normalise(decoded, side):
    row_all, col_all = decoded.shape
    blocks = decoded.reshape(row_all // side, side, col_all // side, side)
    square_mean = jnp.mean(blocks * blocks, axis=(1, 3), keepdims=True)
    return (blocks / jnp.sqrt(square_mean + tiny_eps)).reshape(row_all, col_all)


def local(gradients, momentum, chosen):
    basis = cosine_basis(GROUP)
    side = basis.shape[0]
    own_grad = gradients[0, 0]
    own_momentum = momentum[0]
    group_cols = own_momentum.shape[1] // side
    group_rows = own_momentum.shape[0] // side
    members = lax.axis_size("dev")
    summed = lax.psum_scatter(own_grad.astype(jnp.float32), "dev", scatter_dimension=1, tiled=True)
    spectrum = to_spectrum(decay_rate * own_momentum + summed / members, basis)
    picks = jnp.transpose(chosen, (0, 2, 1, 3))
    pod_index = lax.axis_index("outer")
    own_picks = lax.dynamic_index_in_dim(picks, pod_index, 0, keepdims=False)
    picked = jnp.take_along_axis(spectrum, own_picks, axis=2)
    col_ids = jnp.arange(group_cols, dtype=jnp.int32)[:, None, None]
    row_ids = jnp.arange(group_rows, dtype=jnp.int32)[None, :, None]
    own_table = jnp.zeros_like(spectrum).at[col_ids, row_ids, own_picks].set(picked)
    momentum_out = from_spectrum(spectrum - own_table, basis)[None]
    every_pod = lax.all_gather(picked[None], "outer", axis=0, tiled=True)
    pod_sum = jnp.zeros_like(spectrum).at[col_ids[None], row_ids[None], picks].add(every_pod)
    update = normalise(from_spectrum(pod_sum, basis), side)
    return (momentum_out, update)


def solution(mesh):
    return jax.shard_map(
        local,
        mesh=mesh,
        in_specs=(
            P("outer", "dev", None, None),
            P("outer", None, "dev"),
            P(None, None, "dev", None),
        ),
        out_specs=(P("outer", None, "dev"), P(None, "dev")),
        check_vma=False,
    )
```

profile of v0, /device:TPU:0, one launch (start us, length us, event | category | flops | bytes accessed | tf_op | source)
XLA Modules:
  0.0 337.3 jit_solution(4951322906465013079)
XLA Ops:
  7.2 7.5 %bitcast_convert_fusion = f32[128,20480]{1,0:T(8,128)} fusion(bf16[1,1,128,20480]{3,2,1,0:T(8,128)(2,1)} %param.3), kind=kLoop, calls=%fused_computation.3 | loop fusion | flops 2621440 | bytes 15728640 | tf_op jit(solution)/shard_map/convert_element_type | solution.py:53
  14.8 0.9 copy-done.1
  17.1 178.7 %reduce-scatter.2.cloned.1.call-done = f32[128,2560]{1,0:T(8,128)} async-done(((f32[128,20480]{1,0:T(8,128)}), f32[128,2560]{1,0:T(8,128)}) %reduce-scatter.2.cloned.1.call-update) | async-done | bytes 1310736 | tf_op jit(solution)/shard_map/reduce_scatter | solution.py:53
  195.9 2.6 bitcast_add_fusion
  198.4 1.7 reshape.96
  200.2 2.9 fusion.3
  203.1 3.8 %convolution_bitcast_fusion.1 = f32[40,2,64,64]{3,2,0,1:T(8,128)} fusion(f32[2,40,64,64]{2,3,1,0:T(8,128)S(1)} %fusion.3, f32[64]{0:T(128)S(1)} %get-tuple-element.7, f32[64]{0:T(128)S(1)} %get-tuple-element.6), kind=kOutput, calls=%fused_computation.12 | convolution fusion | flops 251670528 | bytes 2621952 | tf_op jit(solution)/shard_map/ij,rjsk,lk->sril/dot_general | solution.py:26
  206.9 2.3 reshape.97
  209.2 23.9 %gather_fusion = f32[2560]{0:T(1024)S(1)} fusion(f32[40,2,4096]{2,0,1:T(8,128)S(1)} %reshape.97, s32[2560]{0:T(1024)S(1)} %reshape.111), kind=kCustom, calls=%fused_computation | custom fusion | bytes 51200 | tf_op jit(solution)/shard_map/jit(take_along_axis)/gather | solution.py:58
  233.6 10.4 %scatter_custom_fusion = f32[327680]{0:T(1024)S(1)} fusion(s32[2560]{0:T(1024)S(1)} %reshape.117, f32[2560]{0:T(1024)S(1)} %reshape.119, f32[]{:T(128)} %constant.19.clone.1), kind=kCustom, calls=%fused_computation.17 | custom fusion | bytes 1310724
  244.0 1.8 reshape.104
  245.7 3.2 copy_subtract_fusion
  248.9 2.2 reshape.98
  251.2 2.6 fusion.1
  253.8 2.5 convolution_bitcast_fusion
  256.2 1.5 copy.27
  257.8 1.7 broadcast_in_dim_reshape.3
  259.6 5.4 %all_gather.3 = f32[4,40,2,32]{1,3,2,0:T(8,128)S(1)} all-gather(f32[1,40,2,32]{1,3,2,0:T(8,128)S(1)} %copy.29), channel_id=1, replica_groups=mesh['outer'=4,'dev'=8] {'outer'}, dimensions={0}, use_global_device_ids=true | all-gather | bytes 51200 | tf_op jit(solution)/shard_map/all_gather | solution.py:63
  265.3 54.9 %scatter_custom_fusion.1 = f32[327680]{0:T(1024)} fusion(s32[10240]{0:T(1024)S(1)} %reshape.123, f32[10240]{0:T(1024)S(1)} %reshape.125, f32[]{:T(128)} %constant.19.clone.1), kind=kCustom, calls=%fused_computation.15 | custom fusion | flops 10240 | bytes 1310724
  320.2 1.6 reshape.99
  321.8 2.6 fusion.12
  324.4 2.5 fusion
  327.3 1.5 copy.33
  328.8 1.7 reshape.100
  (38 shorter events, 2.5 us)
Async XLA Ops:
  7.2 188.7 %reduce-scatter.2.cloned.1.call-start = ((), (), s32[]{:S(2)}) async-start(), calls=%async_computation.1 | async-start | bytes 11796480 | tf_op jit(solution)/shard_map/reduce_scatter | solution.py:53
  14.7 0.9 copy-start.1
  14.7 1.1 copy-start.3
  14.8 1.3 copy-start.2
  16.0 179.9 %copy-start = (f32[1,128,2560]{2,1,0:T(8,128)S(1)}, f32[1,128,2560]{2,1,0:T(8,128)}, u32[]{:S(2)}) copy-start(f32[1,128,2560]{2,1,0:T(8,128)} %param.4) | copy-start | bytes 3932164
Sparse Core Ops, SparseCore 0:
  14.9 180.9 reduce-scatter.1
where the time goes:
time: 338 us; the launch traced here: 337 us
  waiting for transfers between devices  179 us (53%)
  other arithmetic  69.4 us (21%)
  local copies, waits for them, and re-layouts  52.5 us (16%)
  matrix products  16.9 us (5%)
  between operations  14.3 us (4%)
  blocking collectives  5.41 us (2%)
    reduce_scatter x1, waiting for transfers between devices, local(): lax.psum_scatter(own_grad.astype(jnp.float32), 'dev', scatter_dimension=1...  179 us
    unnamed x7, other arithmetic  55.6 us
    gather x3, local copies, waits for them, and re-layouts, local(): picked = jnp.take_along_axis(spectrum, own_picks, axis=2)  24.1 us
    unnamed x13, local copies, waits for them, and re-layouts  11.8 us
    dot_general x4, matrix products, from_spectrum(): jnp.einsum('ij,sril,lk->rjsk', basis, blocks, basis, precision=lax.Precis...  10.2 us
    convert_element_type x1, other arithmetic, local(): own_grad.astype(jnp.float32)  7.54 us
  transfers between devices with their start and end apart: 1, of which 1 were waited for; matrix products, arithmetic and copies ran while one was open for 0% of the time, Pallas kernels for 0%

commit v1 on v0

v1 whole, which is shorter than its diff:
```python
import functools

import jax
import jax.numpy as jnp
import numpy as np
from jax import lax
from jax.experimental import pallas as pl
from jax.experimental.pallas import tpu as pltpu
from jax.sharding import PartitionSpec as P


GROUP = 64
LANES = 128

decay_rate = 0.999
tiny_eps = 1e-06


VMEM_LIMIT = 16 << 20
bf16 = jnp.bfloat16
f32 = jnp.float32


def cosine_basis(size):
    freq = np.arange(size, dtype=np.float64)[:, None]
    place = np.arange(size, dtype=np.float64)[None, :]
    weight = np.where(freq == 0, np.sqrt(1.0 / size), np.sqrt(2.0 / size))
    return (weight * np.cos(np.pi * (2.0 * place + 1.0) * freq / (2.0 * size))).astype(np.float32)


def halves_of(table):
    high = table.astype(bf16)
    return np.stack([high, (table - high.astype(np.float32)).astype(bf16)])


def split(x):
    high = x.astype(bf16)
    return high, (x - high.astype(f32)).astype(bf16)


def mm(a, b):
    return jnp.dot(a, b, preferred_element_type=f32)


def mm3(x, table):
    high, low = split(x)
    return mm(high, table[0]) + (mm(low, table[0]) + mm(high, table[1]))


def log2(n):
    assert n & (n - 1) == 0
    return n.bit_length() - 1


def table_places(idx, kept, side):
    lane = lax.broadcasted_iota(jnp.int32, idx.shape, 1)
    cell = (lane & (LANES - 1)) >> log2(kept)
    return idx >> log2(side), (cell << log2(side)) + (idx & (side - 1))


def one_hot(hit):
    return jnp.where(hit, 1.0, 0.0).astype(bf16)


def basis_rows(row, tall, side):
    at_row = one_hot(lax.broadcasted_iota(jnp.int32, (side, row.shape[1]), 0) == row)
    return mm(tall[0], at_row) + mm(tall[1], at_row)


def picks_of(xs, places, wide_t, tall, kept, side):
    high, low = split(mm3(jnp.concatenate(xs, axis=0), wide_t))
    found = []
    for i, idx in enumerate(places):
        row, col = table_places(idx, kept, side)
        at_col = one_hot(lax.broadcasted_iota(jnp.int32, (high.shape[1], idx.shape[1]), 0) == col)
        at = slice(i * side, (i + 1) * side)
        cols = mm(high[at], at_col) + mm(low[at], at_col)
        found.append(jnp.sum(cols * basis_rows(row, tall, side), axis=0, keepdims=True))
    return found


def in_vmem(a):
    return pltpu.with_memory_space_constraint(a, pltpu.VMEM)


ON_CHIP = pl.BlockSpec(memory_space=pltpu.VMEM)
PARAMS = pltpu.CompilerParams(vmem_limit_bytes=VMEM_LIMIT)


def cost(flops, moved):
    return pl.CostEstimate(flops=flops, bytes_accessed=moved, transcendentals=0)


def own_kernel(kept, side, members, first, mom_ref, *refs):
    *grad_refs, idx_ref, wide_t_ref, tall_ref, x_ref, v_ref = refs
    parts, count = idx_ref.shape[:2]
    span = wide_t_ref.shape[1]
    spots = [(r, q) for r in range(parts) for q in range(count)]
    xs = []
    for r, q in spots:
        rows = pl.ds(r * side, side)
        x = decay_rate * mom_ref[rows, pl.ds(first + q * span, span)]
        x += grad_refs[r][:, pl.ds(q * span, span)].astype(f32) / members
        x_ref[rows, pl.ds(q * span, span)] = x
        xs.append(x)
    places = [idx_ref[r, pl.ds(q, 1), :] for r, q in spots]
    for (r, q), v in zip(spots, picks_of(xs, places, wide_t_ref, tall_ref, kept, side)):
        v_ref[r, pl.ds(q, 1), :] = v


def own_part(mom, terms, idx, wide_t, tall, kept, side, members, first):
    shape = (mom.shape[0], terms[0].shape[1])
    size = shape[0] * shape[1]
    return pl.pallas_call(
        functools.partial(own_kernel, kept, side, members, first),
        out_shape=(pltpu.VMEM(shape, f32), jax.ShapeDtypeStruct(idx.shape, f32)),
        in_specs=[ON_CHIP] * (len(terms) + 4),
        out_specs=(ON_CHIP, ON_CHIP),
        compiler_params=PARAMS,
        cost_estimate=cost(size * wide_t.shape[1] * 10, size * 10),
    )(in_vmem(mom), *[in_vmem(x) for x in terms], idx, wide_t, tall)


def term_kernel(kept, side, members, *refs):
    *x_refs, idx_ref, wide_t_ref, tall_ref, v_ref = refs
    parts, count = idx_ref.shape[:2]
    span = wide_t_ref.shape[1]
    spots = [(r, q) for r in range(parts) for q in range(count)]
    xs = [x_refs[r][:, pl.ds(q * span, span)].astype(f32) for r, q in spots]
    places = [idx_ref[r, pl.ds(q, 1), :] for r, q in spots]
    for (r, q), v in zip(spots, picks_of(xs, places, wide_t_ref, tall_ref, kept, side)):
        v_ref[r, pl.ds(q, 1), :] = v / members


def term_part(terms, idx, wide_t, tall, kept, side, members):
    return pl.pallas_call(
        functools.partial(term_kernel, kept, side, members),
        out_shape=jax.ShapeDtypeStruct(idx.shape, f32),
        in_specs=[ON_CHIP] * (len(terms) + 3),
        out_specs=ON_CHIP,
        compiler_params=PARAMS,
        cost_estimate=cost(idx.size * side * wide_t.shape[1] * 40, idx.size * side * 4),
    )(*[in_vmem(x) for x in terms], idx, wide_t, tall)


def table_kernel(kept, side, idx_ref, tall_ref, rows_ref, cols_ref):
    pods, parts, count = idx_ref.shape[:3]
    span = cols_ref.shape[3]
    for r in range(parts):
        for q in range(count):
            idx = jnp.concatenate([idx_ref[p, r, pl.ds(q, 1), :] for p in range(pods)], axis=1)
            row, col = table_places(idx, kept, side)
            rows_ref[r, q] = basis_rows(row, tall_ref, side)
            tall_col = jnp.transpose(jnp.broadcast_to(col, (LANES, col.shape[1])))
            for c in range(0, span, LANES):
                lane = lax.broadcasted_iota(jnp.int32, tall_col.shape, 1) + c
                cols_ref[r, q, :, pl.ds(c, LANES)] = one_hot(tall_col == lane)


def table_part(idx, tall, kept, side):
    pods, parts, count, lanes = idx.shape
    span = LANES // kept * side
    return pl.pallas_call(
        functools.partial(table_kernel, kept, side),
        out_shape=(
            pltpu.VMEM((parts, count, side, pods * lanes), f32),
            pltpu.VMEM((parts, count, pods * lanes, span), bf16),
        ),
        in_specs=[ON_CHIP] * 2,
        out_specs=(ON_CHIP, ON_CHIP),
        compiler_params=PARAMS,
        cost_estimate=cost(parts * count * side * side * pods * lanes * 4, parts * count * pods * lanes * span * 2),
    )(idx, tall)


def decode_kernel(side, pod_ref, v_ref, rows_ref, cols_ref, x_ref, wide_ref, same_ref, update_ref, rest_ref, table_ref):
    parts, count, _, lanes = rows_ref.shape
    pods, span = v_ref.shape[0], wide_ref.shape[1]
    mine = (lax.broadcasted_iota(jnp.int32, (1, lanes), 1) >> log2(LANES)) == pod_ref[0]
    for r in range(parts):
        for q in range(count):
            v = jnp.concatenate([v_ref[p, r, pl.ds(q, 1), :] for p in range(pods)], axis=1)
            rows = rows_ref[r, q]
            sides = jnp.concatenate([rows * v, rows * jnp.where(mine, v, 0.0)], axis=0)
            high, low = split(sides)
            table_ref[r * count + q] = mm(high, cols_ref[r, q]) + mm(low, cols_ref[r, q])
    table = table_ref[...].reshape(parts * count * 2 * side, span)
    spatial = mm3(table, wide_ref).reshape(parts * count, 2, side, span)
    shared = spatial[:, 0]
    squares = jnp.sum(shared * shared, axis=1) / (side * side)
    high, low = split(squares)
    mean = mm(high, same_ref[...]) + mm(low, same_ref[...])
    scale = 1.0 / jnp.sqrt(mean + tiny_eps)
    for r in range(parts):
        for q in range(count):
            at = (pl.ds(r * side, side), pl.ds(q * span, span))
            b = r * count + q
            update_ref[at] = shared[b] * scale[b : b + 1, :]
            rest_ref[at] = x_ref[at] - spatial[b, 1]


def decode_part(pod, values, rows, cols, x, wide, same, side):
    parts, count = rows.shape[:2]
    return pl.pallas_call(
        functools.partial(decode_kernel, side),
        out_shape=(pltpu.VMEM(x.shape, f32), pltpu.VMEM(x.shape, f32)),
        in_specs=[pl.BlockSpec(memory_space=pltpu.SMEM)] + [ON_CHIP] * 6,
        out_specs=(ON_CHIP, ON_CHIP),
        scratch_shapes=[pltpu.VMEM((parts * count, 2 * side, wide.shape[1]), f32)],
        compiler_params=PARAMS,
        cost_estimate=cost(x.size * wide.shape[1] * 20, x.size * 12),
    )(pod, values, in_vmem(rows), in_vmem(cols), in_vmem(x), wide, same)


def ring_order(n):
    return [2 * q if q < n // 2 else 2 * n - 1 - 2 * q for q in range(n)]


def ring_at(q, n):
    return jnp.where(q < n // 2, 2 * q, 2 * n - 1 - 2 * q)


CHUNKS = 2


def local(gradients, momentum, chosen, pods, members):
    kept = chosen.shape[3]
    side = GROUP
    per = LANES // kept
    span = per * side
    grad, mom = gradients[0, 0], momentum[0]
    rows, width = mom.shape
    blocks = rows // side
    pod = lax.axis_index("outer")
    me = lax.axis_index("dev")

    basis = cosine_basis(side)
    many = np.kron(np.eye(per, dtype=np.float32), basis)
    wide, wide_t, tall = (jnp.asarray(halves_of(t)) for t in (many, many.T, basis.T))
    same = jnp.asarray(np.kron(np.eye(per), np.ones((side, side))).astype(bf16))
    how = dict(kept=kept, side=side)

    chunks = CHUNKS
    if blocks != 2 or members % 2 or width % (chunks * span):
        summed = lax.psum_scatter(grad.astype(f32), "dev", scatter_dimension=1, tiled=True)
        pad = -width % span
        mom, summed = (jnp.pad(a, ((0, 0), (0, pad))) for a in (mom, summed))
        places = jnp.pad(chosen, ((0, 0), (0, 0), (0, pad // side), (0, 0)))
        count = (width + pad) // span
        places = places.reshape(pods, blocks, count, LANES)
        own_places = lax.dynamic_index_in_dim(places, pod, 0, keepdims=False)
        terms = [summed[r * side : (r + 1) * side] for r in range(blocks)]
        x, v = own_part(mom, terms, own_places, wide_t, tall, members=members, first=0, **how)
        tables = table_part(places, tall, **how)
        every = lax.all_gather(v, "outer")
        update, rest = decode_part(pod[None], every, *tables, x, wide, same, side)
        return rest[None, :, :width], update[:, :width]

    count = width // span
    each = count // chunks
    piece_cols = width // chunks
    ring = ring_order(members)
    position = jnp.where(me % 2 == 0, me // 2, members - 1 - me // 2)

    def ahead(d, steps):
        move = steps if d == 0 else -steps
        return [(ring[i], ring[(i + move) % members]) for i in range(members)]

    def owner(d, s):
        q = position - 1 - s + members if d == 0 else position + 1 + s
        return ring_at(lax.rem(q, members), members)

    def piece(source, d, s, j):
        start = owner(d, s) * width + j * piece_cols
        return lax.dynamic_slice(source, (d * side, start), (side, piece_cols))

    def tie(*arrays):
        return lax.optimization_barrier(arrays)

    def spans(a, j):
        return a[..., j * each : (j + 1) * each, :]

    last = members - 2
    cut = last - 1

    current = [[None] * 2 for _ in range(chunks)]
    token = ()
    for j in range(chunks):
        for d in range(2):
            source, *_ = tie(grad, *token)
            current[j][d] = piece(source, d, 0, j).astype(f32)
            token = (current[j][d],)

    def after(array):
        return tie(array, *token)[0]

    def terms(s, j):
        source = after(grad)
        return [piece(source, d, s, j) for d in range(2)]

    def own_filler(j):
        own[j] = own_part(
            mom,
            terms(members - 1, j),
            after(spans(own_places, j)),
            wide_t,
            tall,
            members=members,
            first=j * piece_cols,
            **how,
        )
        return own[j]

    def near_filler(j):
        raw[j] = term_part(terms(last, j), after(spans(near, j)), wide_t, tall, members=members, **how)
        return (raw[j],)

    def table_filler(j):
        tables[j] = table_part(after(spans(places, j)), tall, **how)
        return tables[j]

    def far_filler(j):
        sent[j] = term_part(current[j], after(spans(far, j)), wide_t, tall, members=members, **how)
        return (sent[j],)

    def moved(both, steps):
        parts = []
        for d in range(2):
            parts.append(lax.ppermute(both[d], "dev", ahead(d, steps)))
        return jnp.stack(parts)

    own, raw, tables, sent = ([None] * chunks for _ in range(4))
    arrivals = [[None] * 2 for _ in range(chunks)]
    fillers = {
        (0, 1): (own_filler, 0),
        (1, 0): (own_filler, 1),
        (1, 1): (near_filler, 0),
        (2, 0): (near_filler, 1),
        (2, 1): (table_filler, 0),
        (3, 0): (table_filler, 1),
        (cut - 1, 0): (far_filler, 0),
        (cut - 1, 1): (far_filler, 1),
    }
    for s in range(members - 1):
        for j in range(chunks):
            for d in range(2):
                arrived = lax.ppermute(current[j][d], "dev", ahead(d, 1))
                if s < last:
                    arrived, source, *_ = tie(arrived, grad, *token)
                    current[j][d] = arrived + piece(source, d, s + 1, j).astype(f32)
                    token = (current[j][d],)
                else:
                    arrivals[j][d] = arrived
            if (s, j) == (0, 0):
                places = after(chosen).reshape(pods, blocks, count, LANES)
                own_places = lax.dynamic_index_in_dim(places, pod, 0, keepdims=False)
                near = moved(own_places, -1)
                far = moved(own_places, -2)
            if (s, j) in fillers:
                fill, i = fillers[s, j]
                token += tuple(fill(i))
            if (s, j) == (2, 0):
                from_near = moved(jnp.concatenate(raw, axis=1), 1)
            if (s, j) == (cut - 1, 1):
                from_far = moved(jnp.concatenate(sent, axis=1), 2)
            if (s, j) == (cut, 1):
                values = jnp.concatenate([v for _, v in own], axis=1) + from_near + from_far
                every = lax.all_gather(after(values), "outer")
                token += (every,)
    updates, outs = [], []
    for j in range(chunks):
        update, rest = decode_part(pod[None], after(spans(every, j)), *tables[j], own[j][0], wide, same, side)
        token = (update,)
        updates.append(update)
        outs.append(rest + jnp.concatenate(arrivals[j], axis=0) / members)
    return jnp.concatenate(outs, axis=1)[None], jnp.concatenate(updates, axis=1)


def solution(mesh):
    def step(*args):
        return local(*args, pods=mesh.shape["outer"], members=mesh.shape["dev"])

    return jax.shard_map(
        step,
        mesh=mesh,
        in_specs=(
            P("outer", "dev", None, None),
            P("outer", None, "dev"),
            P(None, None, "dev", None),
        ),
        out_specs=(P("outer", None, "dev"), P(None, "dev")),
        check_vma=False,
    )
```

time: 338 us -> 124 us (0.37)
  waiting for transfers between devices: 179 us -> 47.3 us
  other arithmetic: 69.4 us -> 14.2 us
  local copies, waits for them, and re-layouts: 52.5 us -> 2.29 us
  starting transfers between devices: 0.04 us -> 41.4 us
  matrix products: 16.9 us -> 0 us
  between operations: 14.3 us -> 1.26 us
  Pallas kernels: 0 us -> 12.3 us
    reduce_scatter x1 -> x0, waiting for transfers between devices: 179 us -> none  [local(): lax.psum_scatter(own_grad.astype(jnp.float32), 'dev', scatter_dimension=1...]
    unnamed x7 -> x0, other arithmetic: 55.6 us -> none
    ppermute x0 -> x36, waiting for transfers between devices: none -> 47.3 us  [the longest x28 46.2 us: local(): arrived = lax.ppermute(current[j][d], 'dev', ahead(d, 1))]
    ppermute x0 -> x36, starting transfers between devices: none -> 41.4 us  [the longest x28 31.6 us: local(): arrived = lax.ppermute(current[j][d], 'dev', ahead(d, 1))]
    gather x3 -> x0, local copies, waits for them, and re-layouts: 24.1 us -> none  [local(): picked = jnp.take_along_axis(spectrum, own_picks, axis=2)]
    dot_general x6 -> x0, matrix products: 16.9 us -> none  [the longest x4 10.2 us: from_spectrum(): jnp.einsum('ij,sril,lk->rjsk', basis, blocks, basis, precision=lax.Precis...]
    pallas_call x0 -> x10, Pallas kernels: none -> 12.3 us  [the longest x4 4.77 us: term_part(): pl.pallas_call(functools.partial(term_kernel, kept, side, members), out_s...]
    unnamed x13 -> x12, local copies, waits for them, and re-layouts: 11.8 us -> 0.04 us
  transfers between devices with their start and end apart: 1 -> 36, of which waited for: 1 -> 15; matrix products, arithmetic and copies ran while one was open for 0% -> 11% of each run, Pallas kernels for 0% -> 10%
where the time goes in v1:
time: 124 us
  waiting for transfers between devices  47.3 us (38%)
  starting transfers between devices  41.4 us (33%)
  other arithmetic  14.2 us (11%)
  Pallas kernels  12.3 us (10%)
  blocking collectives  5.22 us (4%)
  local copies, waits for them, and re-layouts  2.29 us (2%)
  between operations  1.26 us (1%)
    ppermute x28, waiting for transfers between devices, local(): arrived = lax.ppermute(current[j][d], 'dev', ahead(d, 1))  46.2 us
    ppermute x28, starting transfers between devices, local(): arrived = lax.ppermute(current[j][d], 'dev', ahead(d, 1))  31.6 us
    ppermute x8, starting transfers between devices, moved(): parts.append(lax.ppermute(both[d], 'dev', ahead(d, steps)))  9.73 us
    add x24, other arithmetic, local(): current[j][d] = arrived + piece(source, d, s + 1, j).astype(f32)  6.23 us
    convert_element_type x4, other arithmetic, local(): current[j][d] = piece(source, d, 0, j).astype(f32)  5.33 us
    all_gather x1, blocking collectives, local(): every = lax.all_gather(after(values), 'outer')  5.22 us
    pallas_call x4, Pallas kernels, term_part(): pl.pallas_call(functools.partial(term_kernel, kept, side, members), out_s...  4.77 us
    pallas_call x2, Pallas kernels, decode_part(): pl.pallas_call(functools.partial(decode_kernel, side), out_shape=(pltpu.V...  3.32 us
  transfers between devices with their start and end apart: 36, of which 15 were waited for; matrix products, arithmetic and copies ran while one was open for 11% of the time, Pallas kernels for 10%

profile of v1, /device:TPU:0, one launch (start us, length us, event | category | flops | bytes accessed | tf_op | source)
XLA Modules:
  0.0 123.9 jit_solution(4300947577256921982)
XLA Ops:
  1.8 3.1 %collective-permute-start.3 = (f32[64,1280]{1,0:T(8,128)S(1)}, f32[64,1280]{1,0:T(8,128)S(1)}, u32[]{:S(2)}, u32[]{:S(2)}) collective-permute-start(f32[64,1280]{1,0:T(8,128)S(1)} %dynamic-slice_convert_fusion.3), channel_id=1, source_target_pairs={{0,2},{2,4},{4,6},{6,7},{7,5},{5,3},{3,1},{1,0},{8,10},{10,12},{12... | collective-permute-start | bytes 983048 | tf_op jit(solution)/shard_map/ppermute | solution.py:347
  4.9 1.7 %dynamic-slice_convert_fusion.2 = f32[64,1280]{1,0:T(8,128)} fusion(bf16[128,20480]{1,0:T(8,128)(2,1)} %bitcast.33, s32[]{:T(128)S(6)} %select_n.151), kind=kLoop, calls=%fused_computation.32 | loop fusion | flops 81920 | bytes 491524 | tf_op jit(solution)/shard_map/convert_element_type | solution.py:291
  6.5 1.7 %dynamic-slice_convert_fusion.1 = f32[64,1280]{1,0:T(8,128)} fusion(bf16[128,20480]{1,0:T(8,128)(2,1)} %bitcast.34, s32[]{:T(128)S(6)} %select_n.152), kind=kLoop, calls=%fused_computation.31 | loop fusion | flops 81920 | bytes 491524 | tf_op jit(solution)/shard_map/convert_element_type | solution.py:291
  8.2 2.0 %collective-permute-start.1 = (f32[64,1280]{1,0:T(8,128)}, f32[64,1280]{1,0:T(8,128)S(1)}, u32[]{:S(2)}, u32[]{:S(2)}) collective-permute-start(f32[64,1280]{1,0:T(8,128)} %dynamic-slice_convert_fusion.1), channel_id=1, source_target_pairs={{0,2},{2,4},{4,6},{6,7},{7,5},{5,3},{3,1},{1,0},{8,10},{10,12},{12... | collective-permute-start | bytes 983048 | tf_op jit(solution)/shard_map/ppermute | solution.py:347
  11.4 1.9 %collective-permute-done.3 = f32[64,1280]{1,0:T(8,128)S(1)} collective-permute-done((f32[64,1280]{1,0:T(8,128)S(1)}, f32[64,1280]{1,0:T(8,128)S(1)}, u32[]{:S(2)}, u32[]{:S(2)}) %collective-permute-start.3) | collective-permute-done | bytes 327712 | tf_op jit(solution)/shard_map/ppermute | solution.py:347
  13.3 1.7 %convert_add_fusion.23 = f32[64,1280]{1,0:T(8,128)} fusion(f32[64,1280]{1,0:T(8,128)S(1)} %collective-permute-done.3, bf16[128,20480]{1,0:T(8,128)(2,1)} %bitcast.36, s32[]{:T(128)S(6)} %select_n.155), kind=kLoop, calls=%fused_computation.29 | loop fusion | flops 163840 | bytes 819204 | tf_op jit(solution)/shard_map/add | solution.py:350
  15.0 2.4 %collective-permute-done.2 = f32[64,1280]{1,0:T(8,128)} collective-permute-done((f32[64,1280]{1,0:T(8,128)}, f32[64,1280]{1,0:T(8,128)}, u32[]{:S(2)}, u32[]{:S(2)}) %collective-permute-start.2) | collective-permute-done | bytes 327712 | tf_op jit(solution)/shard_map/ppermute | solution.py:347
  19.6 2.6 %collective-permute-start.23 = (s32[10,128]{1,0:T(8,128)S(1)}, s32[10,128]{1,0:T(8,128)S(1)}, u32[]{:S(2)}, u32[]{:S(2)}) collective-permute-start(s32[10,128]{1,0:T(8,128)S(1)} %get-tuple-element.172), channel_id=1, source_target_pairs={{0,4},{2,6},{4,7},{6,5},{7,3},{5,1},{3,0},{1,2},{8,12},{10,14},{12... | collective-permute-start | bytes 15368 | tf_op jit(solution)/shard_map/ppermute | solution.py:329
  33.1 3.4 %collective-permute-done.5 = f32[64,1280]{1,0:T(8,128)S(1)} collective-permute-done((f32[64,1280]{1,0:T(8,128)}, f32[64,1280]{1,0:T(8,128)S(1)}, u32[]{:S(2)}, u32[]{:S(2)}) %collective-permute-start.5) | collective-permute-done | bytes 327712 | tf_op jit(solution)/shard_map/ppermute | solution.py:347
  39.1 4.9 %collective-permute-done.4 = f32[64,1280]{1,0:T(8,128)S(1)} collective-permute-done((f32[64,1280]{1,0:T(8,128)S(1)}, f32[64,1280]{1,0:T(8,128)S(1)}, u32[]{:S(2)}, u32[]{:S(2)}) %collective-permute-start.4) | collective-permute-done | bytes 327712 | tf_op jit(solution)/shard_map/ppermute | solution.py:347
  50.3 10.0 %collective-permute-done.10 = f32[64,1280]{1,0:T(8,128)S(1)} collective-permute-done((f32[64,1280]{1,0:T(8,128)S(1)}, f32[64,1280]{1,0:T(8,128)S(1)}, u32[]{:S(2)}, u32[]{:S(2)}) %collective-permute-start.10) | collective-permute-done | bytes 327712 | tf_op jit(solution)/shard_map/ppermute | solution.py:347
  68.3 3.1 %collective-permute-done.14 = f32[64,1280]{1,0:T(8,128)S(1)} collective-permute-done((f32[64,1280]{1,0:T(8,128)S(1)}, f32[64,1280]{1,0:T(8,128)S(1)}, u32[]{:S(2)}, u32[]{:S(2)}) %collective-permute-start.14) | collective-permute-done | bytes 327712 | tf_op jit(solution)/shard_map/ppermute | solution.py:347
  71.5 1.7 %collective-permute-start.21 = (f32[64,1280]{1,0:T(8,128)S(1)}, f32[64,1280]{1,0:T(8,128)S(1)}, u32[]{:S(2)}, u32[]{:S(2)}) collective-permute-start(f32[64,1280]{1,0:T(8,128)S(1)} %convert_add_fusion.10), channel_id=1, source_target_pairs={{0,1},{2,0},{4,2},{6,4},{7,6},{5,7},{3,5},{1,3},{8,9},{10,8},{12,1... | collective-permute-start | bytes 983048 | tf_op jit(solution)/shard_map/ppermute | solution.py:347
  74.1 4.3 %collective-permute-done.19 = f32[64,1280]{1,0:T(8,128)S(1)} collective-permute-done((f32[64,1280]{1,0:T(8,128)S(1)}, f32[64,1280]{1,0:T(8,128)S(1)}, u32[]{:S(2)}, u32[]{:S(2)}) %collective-permute-start.19) | collective-permute-done | bytes 327712 | tf_op jit(solution)/shard_map/ppermute | solution.py:347
  81.7 3.8 %collective-permute-done.17 = f32[64,1280]{1,0:T(8,128)S(1)} collective-permute-done((f32[64,1280]{1,0:T(8,128)S(1)}, f32[64,1280]{1,0:T(8,128)S(1)}, u32[]{:S(2)}, u32[]{:S(2)}) %collective-permute-start.17) | collective-permute-done | bytes 327712 | tf_op jit(solution)/shard_map/ppermute | solution.py:347
  85.7 1.9 %collective-permute-start.31 = (f32[64,1280]{1,0:T(8,128)S(1)}, f32[64,1280]{1,0:T(8,128)S(1)}, u32[]{:S(2)}, u32[]{:S(2)}) collective-permute-start(f32[64,1280]{1,0:T(8,128)S(1)} %convert_add_fusion.7.refs_0_), channel_id=1, source_target_pairs={{0,2},{2,4},{4,6},{6,7},{7,5},{5,3},{3,1},{1,0},{8,10},{10,12},{12... | collective-permute-start | bytes 983048 | tf_op jit(solution)/shard_map/ppermute | solution.py:347
  89.6 6.5 %collective-permute-done.25 = f32[64,1280]{1,0:T(8,128)S(1)} collective-permute-done((f32[64,1280]{1,0:T(8,128)S(1)}, f32[64,1280]{1,0:T(8,128)S(1)}, u32[]{:S(2)}, u32[]{:S(2)}) %collective-permute-start.25) | collective-permute-done | bytes 327712 | tf_op jit(solution)/shard_map/ppermute | solution.py:347
  97.3 2.9 %collective-permute-start.26 = (f32[10,128]{1,0:T(8,128)S(1)}, f32[10,128]{1,0:T(8,128)S(1)}, u32[]{:S(2)}, u32[]{:S(2)}) collective-permute-start(f32[10,128]{1,0:T(8,128)S(1)} %get-tuple-element.174), channel_id=1, source_target_pairs={{0,4},{2,6},{4,7},{6,5},{7,3},{5,1},{3,0},{1,2},{8,12},{10,14},{12... | collective-permute-start | bytes 15368 | tf_op jit(solution)/shard_map/ppermute | solution.py:329
  100.7 1.9 %collective-permute-start.28 = (f32[64,1280]{1,0:T(8,128)S(1)}, f32[64,1280]{1,0:T(8,128)S(1)}, u32[]{:S(2)}, u32[]{:S(2)}) collective-permute-start(f32[64,1280]{1,0:T(8,128)S(1)} %convert_add_fusion.4.refs_1_), channel_id=1, source_target_pairs={{0,1},{2,0},{4,2},{6,4},{7,6},{5,7},{3,5},{1,3},{8,9},{10,8},{12,1... | collective-permute-start | bytes 983048 | tf_op jit(solution)/shard_map/ppermute | solution.py:347
  104.9 1.6 %collective-permute-start.32 = (f32[64,1280]{1,0:T(8,128)S(1)}, f32[64,1280]{1,0:T(8,128)S(1)}, u32[]{:S(2)}, u32[]{:S(2)}) collective-permute-start(f32[64,1280]{1,0:T(8,128)S(1)} %convert_add_fusion.3), channel_id=1, source_target_pairs={{0,2},{2,4},{4,6},{6,7},{7,5},{5,3},{3,1},{1,0},{8,10},{10,12},{12... | collective-permute-start | bytes 983048 | tf_op jit(solution)/shard_map/ppermute | solution.py:347
  106.5 2.3 %collective-permute-done.30 = f32[64,1280]{1,0:T(8,128)S(1)} collective-permute-done((f32[64,1280]{1,0:T(8,128)S(1)}, f32[64,1280]{1,0:T(8,128)S(1)}, u32[]{:S(2)}, u32[]{:S(2)}) %collective-permute-start.30) | collective-permute-done | bytes 327712 | tf_op jit(solution)/shard_map/ppermute | solution.py:347
  112.7 5.2 %all-gather = f32[8,10,128]{2,1,0:T(8,128)S(1)} all-gather(f32[2,10,128]{2,1,0:T(8,128)S(1)} %fusion.2), channel_id=2, replica_groups=mesh['outer'=4,'dev'=8] {'outer'}, dimensions={0}, use_global_device_ids=true | all-gather | bytes 51200 | tf_op jit(solution)/shard_map/all_gather | solution.py:368
  118.0 1.7 %shard_map.94 = (f32[128,1280]{1,0:T(8,128)S(1)}, f32[128,1280]{1,0:T(8,128)S(1)}) custom-call(s32[1]{0:T(128)} %bitcast.pod_ref, f32[4,2,5,128]{3,2,1,0:T(8,128)S(1)} %get-tuple-element.154.v_ref, f32[2,5,64,512]{3,2,1,0:T(8,128)S(1)} %get-tuple-element.122.rows_ref, bf16[2,5,512,256]{3,2,1,0:T(8,128)(2,1)S(1)} %get-tuple-element.123.cols_ref, ...), custom_call_target="tpu_custom_call" | custom-call | flops 838860800 | bytes 1966080 | tf_op jit(solution)/shard_map/pallas_call | solution.py:204
  119.6 1.7 %shard_map.95 = (f32[128,1280]{1,0:T(8,128)S(1)}, f32[128,1280]{1,0:T(8,128)S(1)}) custom-call(s32[1]{0:T(128)} %bitcast.pod_ref, f32[4,2,5,128]{3,2,1,0:T(8,128)S(1)} %get-tuple-element.157.v_ref, f32[2,5,64,512]{3,2,1,0:T(8,128)S(1)} %get-tuple-element.129.rows_ref, bf16[2,5,512,256]{3,2,1,0:T(8,128)(2,1)S(1)} %get-tuple-element.130.cols_ref, ...), custom_call_target="tpu_custom_call" | custom-call | flops 838860800 | bytes 1966080 | tf_op jit(solution)/shard_map/pallas_call | solution.py:204
  (119 shorter events, 48.7 us)
Async XLA Ops:
  1.8 11.6 %collective-permute-start.3 = (f32[64,1280]{1,0:T(8,128)S(1)}, f32[64,1280]{1,0:T(8,128)S(1)}, u32[]{:S(2)}, u32[]{:S(2)}) collective-permute-start(f32[64,1280]{1,0:T(8,128)S(1)} %dynamic-slice_convert_fusion.3), channel_id=1, source_target_pairs={{0,2},{2,4},{4,6},{6,7},{7,5},{5,3},{3,1},{1,0},{8,10},{10,12},{12... | collective-permute-start | bytes 983048 | tf_op jit(solution)/shard_map/ppermute | solution.py:347
  6.5 10.9 %collective-permute-start.2 = (f32[64,1280]{1,0:T(8,128)}, f32[64,1280]{1,0:T(8,128)}, u32[]{:S(2)}, u32[]{:S(2)}) collective-permute-start(f32[64,1280]{1,0:T(8,128)} %dynamic-slice_convert_fusion.2), channel_id=1, source_target_pairs={{0,1},{2,0},{4,2},{6,4},{7,6},{5,7},{3,5},{1,3},{8,9},{10,8},{12,1... | collective-permute-start | bytes 983048 | tf_op jit(solution)/shard_map/ppermute | solution.py:347
  8.2 16.0 %collective-permute-start.1 = (f32[64,1280]{1,0:T(8,128)}, f32[64,1280]{1,0:T(8,128)S(1)}, u32[]{:S(2)}, u32[]{:S(2)}) collective-permute-start(f32[64,1280]{1,0:T(8,128)} %dynamic-slice_convert_fusion.1), channel_id=1, source_target_pairs={{0,2},{2,4},{4,6},{6,7},{7,5},{5,3},{3,1},{1,0},{8,10},{10,12},{12... | collective-permute-start | bytes 983048 | tf_op jit(solution)/shard_map/ppermute | solution.py:347
  11.2 14.4 %collective-permute-start = (f32[64,1280]{1,0:T(8,128)S(1)}, f32[64,1280]{1,0:T(8,128)S(1)}, u32[]{:S(2)}, u32[]{:S(2)}) collective-permute-start(f32[64,1280]{1,0:T(8,128)S(1)} %dynamic-slice_convert_fusion), channel_id=1, source_target_pairs={{0,1},{2,0},{4,2},{6,4},{7,6},{5,7},{3,5},{1,3},{8,9},{10,8},{12,1... | collective-permute-start | bytes 983048 | tf_op jit(solution)/shard_map/ppermute | solution.py:347
  19.6 10.9 %collective-permute-start.23 = (s32[10,128]{1,0:T(8,128)S(1)}, s32[10,128]{1,0:T(8,128)S(1)}, u32[]{:S(2)}, u32[]{:S(2)}) collective-permute-start(s32[10,128]{1,0:T(8,128)S(1)} %get-tuple-element.172), channel_id=1, source_target_pairs={{0,4},{2,6},{4,7},{6,5},{7,3},{5,1},{3,0},{1,2},{8,12},{10,14},{12... | collective-permute-start | bytes 15368 | tf_op jit(solution)/shard_map/ppermute | solution.py:329
  25.6 10.8 %collective-permute-start.5 = (f32[64,1280]{1,0:T(8,128)}, f32[64,1280]{1,0:T(8,128)S(1)}, u32[]{:S(2)}, u32[]{:S(2)}) collective-permute-start(f32[64,1280]{1,0:T(8,128)} %convert_add_fusion.23), channel_id=1, source_target_pairs={{0,2},{2,4},{4,6},{6,7},{7,5},{5,3},{3,1},{1,0},{8,10},{10,12},{12... | collective-permute-start | bytes 983048 | tf_op jit(solution)/shard_map/ppermute | solution.py:347
  30.5 14.9 %collective-permute-start.6 = (f32[64,1280]{1,0:T(8,128)S(1)}, f32[64,1280]{1,0:T(8,128)S(1)}, u32[]{:S(2)}, u32[]{:S(2)}) collective-permute-start(f32[64,1280]{1,0:T(8,128)S(1)} %convert_add_fusion.20), channel_id=1, source_target_pairs={{0,1},{2,0},{4,2},{6,4},{7,6},{5,7},{3,5},{1,3},{8,9},{10,8},{12,1... | collective-permute-start | bytes 983048 | tf_op jit(solution)/shard_map/ppermute | solution.py:347
  31.0 14.3 %collective-permute-start.7 = (f32[64,1280]{1,0:T(8,128)S(1)}, f32[64,1280]{1,0:T(8,128)S(1)}, u32[]{:S(2)}, u32[]{:S(2)}) collective-permute-start(f32[64,1280]{1,0:T(8,128)S(1)} %convert_add_fusion.21), channel_id=1, source_target_pairs={{0,2},{2,4},{4,6},{6,7},{7,5},{5,3},{3,1},{1,0},{8,10},{10,12},{12... | collective-permute-start | bytes 983048 | tf_op jit(solution)/shard_map/ppermute | solution.py:347
  32.6 11.4 %collective-permute-start.4 = (f32[64,1280]{1,0:T(8,128)S(1)}, f32[64,1280]{1,0:T(8,128)S(1)}, u32[]{:S(2)}, u32[]{:S(2)}) collective-permute-start(f32[64,1280]{1,0:T(8,128)S(1)} %convert_add_fusion.22), channel_id=1, source_target_pairs={{0,1},{2,0},{4,2},{6,4},{7,6},{5,7},{3,5},{1,3},{8,9},{10,8},{12,1... | collective-permute-start | bytes 983048 | tf_op jit(solution)/shard_map/ppermute | solution.py:347
  37.4 12.8 %collective-permute-start.11 = (f32[64,1280]{1,0:T(8,128)S(1)}, f32[64,1280]{1,0:T(8,128)S(1)}, u32[]{:S(2)}, u32[]{:S(2)}) collective-permute-start(f32[64,1280]{1,0:T(8,128)S(1)} %convert_add_fusion.19), channel_id=1, source_target_pairs={{0,2},{2,4},{4,6},{6,7},{7,5},{5,3},{3,1},{1,0},{8,10},{10,12},{12... | collective-permute-start | bytes 983048 | tf_op jit(solution)/shard_map/ppermute | solution.py:347
  45.4 19.9 %collective-permute-start.15 = (f32[64,1280]{1,0:T(8,128)S(1)}, f32[64,1280]{1,0:T(8,128)S(1)}, u32[]{:S(2)}, u32[]{:S(2)}) collective-permute-start(f32[64,1280]{1,0:T(8,128)S(1)} %convert_add_fusion.16), channel_id=1, source_target_pairs={{0,1},{2,0},{4,2},{6,4},{7,6},{5,7},{3,5},{1,3},{8,9},{10,8},{12,1... | collective-permute-start | bytes 983048 | tf_op jit(solution)/shard_map/ppermute | solution.py:347
  45.9 17.7 %collective-permute-start.16 = (f32[64,1280]{1,0:T(8,128)S(1)}, f32[64,1280]{1,0:T(8,128)S(1)}, u32[]{:S(2)}, u32[]{:S(2)}) collective-permute-start(f32[64,1280]{1,0:T(8,128)S(1)} %convert_add_fusion.17), channel_id=1, source_target_pairs={{0,2},{2,4},{4,6},{6,7},{7,5},{5,3},{3,1},{1,0},{8,10},{10,12},{12... | collective-permute-start | bytes 983048 | tf_op jit(solution)/shard_map/ppermute | solution.py:347
  47.5 12.8 %collective-permute-start.10 = (f32[64,1280]{1,0:T(8,128)S(1)}, f32[64,1280]{1,0:T(8,128)S(1)}, u32[]{:S(2)}, u32[]{:S(2)}) collective-permute-start(f32[64,1280]{1,0:T(8,128)S(1)} %convert_add_fusion.18), channel_id=1, source_target_pairs={{0,1},{2,0},{4,2},{6,4},{7,6},{5,7},{3,5},{1,3},{8,9},{10,8},{12,1... | collective-permute-start | bytes 983048 | tf_op jit(solution)/shard_map/ppermute | solution.py:347
  60.3 11.1 %collective-permute-start.20 = (f32[64,1280]{1,0:T(8,128)S(1)}, f32[64,1280]{1,0:T(8,128)S(1)}, u32[]{:S(2)}, u32[]{:S(2)}) collective-permute-start(f32[64,1280]{1,0:T(8,128)S(1)} %convert_add_fusion.14), channel_id=1, source_target_pairs={{0,1},{2,0},{4,2},{6,4},{7,6},{5,7},{3,5},{1,3},{8,9},{10,8},{12,1... | collective-permute-start | bytes 983048 | tf_op jit(solution)/shard_map/ppermute | solution.py:347
  63.6 14.8 %collective-permute-start.19 = (f32[64,1280]{1,0:T(8,128)S(1)}, f32[64,1280]{1,0:T(8,128)S(1)}, u32[]{:S(2)}, u32[]{:S(2)}) collective-permute-start(f32[64,1280]{1,0:T(8,128)S(1)} %convert_add_fusion.13), channel_id=1, source_target_pairs={{0,2},{2,4},{4,6},{6,7},{7,5},{5,3},{3,1},{1,0},{8,10},{10,12},{12... | collective-permute-start | bytes 983048 | tf_op jit(solution)/shard_map/ppermute | solution.py:347
  65.3 14.7 %collective-permute-start.18 = (f32[64,1280]{1,0:T(8,128)S(1)}, f32[64,1280]{1,0:T(8,128)S(1)}, u32[]{:S(2)}, u32[]{:S(2)}) collective-permute-start(f32[64,1280]{1,0:T(8,128)S(1)} %convert_add_fusion.12), channel_id=1, source_target_pairs={{0,1},{2,0},{4,2},{6,4},{7,6},{5,7},{3,5},{1,3},{8,9},{10,8},{12,1... | collective-permute-start | bytes 983048 | tf_op jit(solution)/shard_map/ppermute | solution.py:347
  65.8 34.6 %collective-permute-start.12 = (f32[10,128]{1,0:T(8,128)S(1)}, f32[10,128]{1,0:T(8,128)S(1)}, u32[]{:S(2)}, u32[]{:S(2)}) collective-permute-start(f32[10,128]{1,0:T(8,128)S(1)} %get-tuple-element.178), channel_id=1, source_target_pairs={{0,2},{2,4},{4,6},{6,7},{7,5},{5,3},{3,1},{1,0},{8,10},{10,12},{12... | collective-permute-start | bytes 15368 | tf_op jit(solution)/shard_map/ppermute | solution.py:329
  71.4 29.3 %collective-permute-start.13 = (f32[10,128]{1,0:T(8,128)S(1)}, f32[10,128]{1,0:T(8,128)S(1)}, u32[]{:S(2)}, u32[]{:S(2)}) collective-permute-start(f32[10,128]{1,0:T(8,128)S(1)} %get-tuple-element.179), channel_id=1, source_target_pairs={{0,1},{2,0},{4,2},{6,4},{7,6},{5,7},{3,5},{1,3},{8,9},{10,8},{12,1... | collective-permute-start | bytes 15368 | tf_op jit(solution)/shard_map/ppermute | solution.py:329
  71.5 14.2 %collective-permute-start.21 = (f32[64,1280]{1,0:T(8,128)S(1)}, f32[64,1280]{1,0:T(8,128)S(1)}, u32[]{:S(2)}, u32[]{:S(2)}) collective-permute-start(f32[64,1280]{1,0:T(8,128)S(1)} %convert_add_fusion.10), channel_id=1, source_target_pairs={{0,1},{2,0},{4,2},{6,4},{7,6},{5,7},{3,5},{1,3},{8,9},{10,8},{12,1... | collective-permute-start | bytes 983048 | tf_op jit(solution)/shard_map/ppermute | solution.py:347
  85.7 19.2 %collective-permute-start.31 = (f32[64,1280]{1,0:T(8,128)S(1)}, f32[64,1280]{1,0:T(8,128)S(1)}, u32[]{:S(2)}, u32[]{:S(2)}) collective-permute-start(f32[64,1280]{1,0:T(8,128)S(1)} %convert_add_fusion.7.refs_0_), channel_id=1, source_target_pairs={{0,2},{2,4},{4,6},{6,7},{7,5},{5,3},{3,1},{1,0},{8,10},{10,12},{12... | collective-permute-start | bytes 983048 | tf_op jit(solution)/shard_map/ppermute | solution.py:347
  100.7 11.6 %collective-permute-start.28 = (f32[64,1280]{1,0:T(8,128)S(1)}, f32[64,1280]{1,0:T(8,128)S(1)}, u32[]{:S(2)}, u32[]{:S(2)}) collective-permute-start(f32[64,1280]{1,0:T(8,128)S(1)} %convert_add_fusion.4.refs_1_), channel_id=1, source_target_pairs={{0,1},{2,0},{4,2},{6,4},{7,6},{5,7},{3,5},{1,3},{8,9},{10,8},{12,1... | collective-permute-start | bytes 983048 | tf_op jit(solution)/shard_map/ppermute | solution.py:347
  104.9 17.6 %collective-permute-start.32 = (f32[64,1280]{1,0:T(8,128)S(1)}, f32[64,1280]{1,0:T(8,128)S(1)}, u32[]{:S(2)}, u32[]{:S(2)}) collective-permute-start(f32[64,1280]{1,0:T(8,128)S(1)} %convert_add_fusion.3), channel_id=1, source_target_pairs={{0,2},{2,4},{4,6},{6,7},{7,5},{5,3},{3,1},{1,0},{8,10},{10,12},{12... | collective-permute-start | bytes 983048 | tf_op jit(solution)/shard_map/ppermute | solution.py:347
  108.8 13.6 %collective-permute-start.33 = (f32[64,1280]{1,0:T(8,128)S(1)}, f32[64,1280]{1,0:T(8,128)S(1)}, u32[]{:S(2)}, u32[]{:S(2)}) collective-permute-start(f32[64,1280]{1,0:T(8,128)S(1)} %convert_add_fusion.2), channel_id=1, source_target_pairs={{0,1},{2,0},{4,2},{6,4},{7,6},{5,7},{3,5},{1,3},{8,9},{10,8},{12,1... | collective-permute-start | bytes 983048 | tf_op jit(solution)/shard_map/ppermute | solution.py:347
  109.7 12.9 %collective-permute-start.34 = (f32[64,1280]{1,0:T(8,128)S(1)}, f32[64,1280]{1,0:T(8,128)S(1)}, u32[]{:S(2)}, u32[]{:S(2)}) collective-permute-start(f32[64,1280]{1,0:T(8,128)S(1)} %convert_add_fusion.1), channel_id=1, source_target_pairs={{0,2},{2,4},{4,6},{6,7},{7,5},{5,3},{3,1},{1,0},{8,10},{10,12},{12... | collective-permute-start | bytes 983048 | tf_op jit(solution)/shard_map/ppermute | solution.py:347
  (18 other events, 270.7 us)

commit v2 on v1

--- a/solution.py
+++ b/solution.py
@@ -77,6 +77,10 @@
         cols = mm(high[at], at_col) + mm(low[at], at_col)
         found.append(jnp.sum(cols * basis_rows(row, tall, side), axis=0, keepdims=True))
     return found
+
+
+def in_hbm(a):
+    return pltpu.with_memory_space_constraint(a, pltpu.HBM)
 
 
 def in_vmem(a):
@@ -173,13 +177,15 @@
     )(idx, tall)
 
 
-def decode_kernel(side, pod_ref, v_ref, rows_ref, cols_ref, x_ref, wide_ref, same_ref, update_ref, rest_ref, table_ref):
+def decode_kernel(side, chunk, pod_ref, v_ref, rows_ref, cols_ref, x_ref, wide_ref, same_ref, *refs):
+    update_hbm, rest_ref, table_ref, update_ref, sem_ref = refs[-5:]
     parts, count, _, lanes = rows_ref.shape
     pods, span = v_ref.shape[0], wide_ref.shape[1]
     mine = (lax.broadcasted_iota(jnp.int32, (1, lanes), 1) >> log2(LANES)) == pod_ref[0]
     for r in range(parts):
         for q in range(count):
-            v = jnp.concatenate([v_ref[p, r, pl.ds(q, 1), :] for p in range(pods)], axis=1)
+            at = pl.ds(chunk * count + q, 1)
+            v = jnp.concatenate([v_ref[p, r, at, :] for p in range(pods)], axis=1)
             rows = rows_ref[r, q]
             sides = jnp.concatenate([rows * v, rows * jnp.where(mine, v, 0.0)], axis=0)
             high, low = split(sides)
@@ -193,34 +199,117 @@
     scale = 1.0 / jnp.sqrt(mean + tiny_eps)
     for r in range(parts):
         for q in range(count):
-            at = (pl.ds(r * side, side), pl.ds(q * span, span))
-            b = r * count + q
+            at, b = (pl.ds(r * side, side), pl.ds(q * span, span)), r * count + q
             update_ref[at] = shared[b] * scale[b : b + 1, :]
+    columns = pl.ds(chunk * update_ref.shape[1], update_ref.shape[1])
+    copy = pltpu.make_async_copy(update_ref, update_hbm.at[:, columns], sem_ref)
+    copy.start()
+    for r in range(parts):
+        for q in range(count):
+            at, b = (pl.ds(r * side, side), pl.ds(q * span, span)), r * count + q
             rest_ref[at] = x_ref[at] - spatial[b, 1]
-
-
-def decode_part(pod, values, rows, cols, x, wide, same, side):
+    copy.wait()
+
+
+def decode_part(pod, values, tables, x, wide, same, side, chunk, chunks, update):
+    rows, cols = tables
     parts, count = rows.shape[:2]
-    return pl.pallas_call(
-        functools.partial(decode_kernel, side),
-        out_shape=(pltpu.VMEM(x.shape, f32), pltpu.VMEM(x.shape, f32)),
-        in_specs=[pl.BlockSpec(memory_space=pltpu.SMEM)] + [ON_CHIP] * 6,
-        out_specs=(ON_CHIP, ON_CHIP),
-        scratch_shapes=[pltpu.VMEM((parts * count, 2 * side, wide.shape[1]), f32)],
-        compiler_params=PARAMS,
-        cost_estimate=cost(x.size * wide.shape[1] * 20, x.size * 12),
-    )(pod, values, in_vmem(rows), in_vmem(cols), in_vmem(x), wide, same)
+    height, width = x.shape
+    held = [] if update is None else [update]
+    hbm = pl.BlockSpec(memory_space=pl.ANY)
+    return pl.pallas_call(
+        functools.partial(decode_kernel, side, chunk),
+        out_shape=(jax.ShapeDtypeStruct((height, chunks * width), f32), pltpu.VMEM(x.shape, f32)),
+        in_specs=[pl.BlockSpec(memory_space=pltpu.SMEM)] + [ON_CHIP] * 6 + [hbm] * len(held),
+        out_specs=(hbm, ON_CHIP),
+        scratch_shapes=[
+            pltpu.VMEM((parts * count, 2 * side, wide.shape[2]), f32),
+            pltpu.VMEM(x.shape, f32),
+            pltpu.SemaphoreType.DMA,
+        ],
+        input_output_aliases={7: 0} if held else {},
+        compiler_params=PARAMS,
+        cost_estimate=cost(x.size * wide.shape[2] * 20, x.size * 12),
+    )(pod, values, in_vmem(rows), in_vmem(cols), in_vmem(x), wide, same, *held)
+
+
+def finish_kernel(members, first, ways, rest_ref, *refs):
+    arrived_refs, (out_ref, buffer_ref, sem_ref) = refs[:ways], refs[-3:]
+    height, width = arrived_refs[0].shape
+    copies = []
+    for d, arrived_ref in enumerate(arrived_refs):
+        rows = pl.ds(d * height, height)
+        buffer_ref[rows, :] = rest_ref[rows, :] + arrived_ref[...] / members
+        target = out_ref.at[rows, pl.ds(first, width)]
+        copies.append(pltpu.make_async_copy(buffer_ref.at[rows], target, sem_ref.at[d]))
+        copies[-1].start()
+    for copy in copies:
+        copy.wait()
+
+
+def finish_part(out, columns, rest, arrived, members, first):
+    held = [] if out is None else [out]
+    hbm = pl.BlockSpec(memory_space=pl.ANY)
+    return pl.pallas_call(
+        functools.partial(finish_kernel, members, first, len(arrived)),
+        out_shape=jax.ShapeDtypeStruct((rest.shape[0], columns), f32),
+        in_specs=[ON_CHIP] * (1 + len(arrived)) + [hbm] * len(held),
+        out_specs=hbm,
+        scratch_shapes=[pltpu.VMEM(rest.shape, f32), pltpu.SemaphoreType.DMA((len(arrived),))],
+        input_output_aliases={1 + len(arrived): 0} if held else {},
+        compiler_params=PARAMS,
+        cost_estimate=cost(rest.size, rest.size * 12),
+    )(in_vmem(rest), *[in_vmem(a) for a in arrived], *held)
+
+
+def ring_position(members):
+    me = lax.axis_index("dev")
+    return jnp.where((me & 1) == 0, me >> 1, members - 1 - (me >> 1))
+
+
+def ring_owner(position, d, s, members):
+    q = position - 1 - s if d == 0 else position + 1 + s
+    q = jnp.where(q < 0, q + members, jnp.where(q >= members, q - members, q))
+    return jnp.where(q < members // 2, 2 * q, 2 * members - 1 - 2 * q)
+
+
+def load_kernel(members, side, j, s, ways, grad_ref, *refs):
+    out_refs, (buffer_ref, sem_ref) = refs[-2 - len(ways) : -2], refs[-2:]
+    arrived_refs = refs[: -2 - len(ways)]
+    width = out_refs[0].shape[1]
+    position = ring_position(members)
+    chunks = grad_ref.shape[1] // (members * width)
+    copies = []
+    for i, d in enumerate(ways):
+        start = pl.multiple_of((ring_owner(position, d, s, members) * chunks + j) * width, LANES)
+        source = grad_ref.at[pl.ds(d * side, side), pl.ds(start, width)]
+        copies.append(pltpu.make_async_copy(source, buffer_ref.at[i], sem_ref.at[i]))
+        copies[-1].start()
+    for i, copy in enumerate(copies):
+        copy.wait()
+        term = buffer_ref[i].astype(f32)
+        out_refs[i][...] = arrived_refs[i][...] + term if arrived_refs else term
+
+
+def load_part(grad, arrived, ways, j, s, members, side, width):
+    return pl.pallas_call(
+        functools.partial(load_kernel, members, side, j, s, ways),
+        out_shape=[pltpu.VMEM((side, width), f32) for _ in ways],
+        in_specs=[pl.BlockSpec(memory_space=pl.ANY)] + [ON_CHIP] * len(arrived),
+        out_specs=[ON_CHIP] * len(ways),
+        scratch_shapes=[pltpu.VMEM((len(ways), side, width), grad.dtype), pltpu.SemaphoreType.DMA((len(ways),))],
+        compiler_params=PARAMS,
+        cost_estimate=cost(side * width, side * width * 6),
+    )(grad, *[in_vmem(a) for a in arrived])
 
 
 def ring_order(n):
     return [2 * q if q < n // 2 else 2 * n - 1 - 2 * q for q in range(n)]
 
 
-def ring_at(q, n):
-    return jnp.where(q < n // 2, 2 * q, 2 * n - 1 - 2 * q)
-
-
 CHUNKS = 2
+HOPS = 3
+LEAST_RING = HOPS + 5
 
 
 def local(gradients, momentum, chosen, pods, members):
@@ -232,7 +321,6 @@
     rows, width = mom.shape
     blocks = rows // side
     pod = lax.axis_index("outer")
-    me = lax.axis_index("dev")
 
     basis = cosine_basis(side)
     many = np.kron(np.eye(per, dtype=np.float32), basis)
@@ -241,7 +329,7 @@
     how = dict(kept=kept, side=side)
 
     chunks = CHUNKS
-    if blocks != 2 or members % 2 or width % (chunks * span):
+    if blocks != 2 or members % 2 or members < LEAST_RING or width % (chunks * span):
         summed = lax.psum_scatter(grad.astype(f32), "dev", scatter_dimension=1, tiled=True)
         pad = -width % span
         mom, summed = (jnp.pad(a, ((0, 0), (0, pad))) for a in (mom, summed))
@@ -253,26 +341,25 @@
         x, v = own_part(mom, terms, own_places, wide_t, tall, members=members, first=0, **how)
         tables = table_part(places, tall, **how)
         every = lax.all_gather(v, "outer")
-        update, rest = decode_part(pod[None], every, *tables, x, wide, same, side)
+        update, rest = decode_part(pod[None], every, tables, x, wide, same, side, 0, 1, None)
         return rest[None, :, :width], update[:, :width]
 
     count = width // span
     each = count // chunks
     piece_cols = width // chunks
     ring = ring_order(members)
-    position = jnp.where(me % 2 == 0, me // 2, members - 1 - me // 2)
+    position = ring_position(members)
 
     def ahead(d, steps):
         move = steps if d == 0 else -steps
         return [(ring[i], ring[(i + move) % members]) for i in range(members)]
 
-    def owner(d, s):
-        q = position - 1 - s + members if d == 0 else position + 1 + s
-        return ring_at(lax.rem(q, members), members)
-
     def piece(source, d, s, j):
-        start = owner(d, s) * width + j * piece_cols
+        start = ring_owner(position, d, s, members) * width + j * piece_cols
         return lax.dynamic_slice(source, (d * side, start), (side, piece_cols))
+
+    def load(source, arrived, ways, j, s):
+        return load_part(source, arrived, ways, j, s, members, side, piece_cols)
 
     def tie(*arrays):
         return lax.optimization_barrier(arrays)
@@ -281,18 +368,26 @@
         return a[..., j * each : (j + 1) * each, :]
 
     last = members - 2
-    cut = last - 1
+    send = last + 1 - HOPS
 
     current = [[None] * 2 for _ in range(chunks)]
     token = ()
     for j in range(chunks):
-        for d in range(2):
-            source, *_ = tie(grad, *token)
-            current[j][d] = piece(source, d, 0, j).astype(f32)
-            token = (current[j][d],)
+        current[j] = list(load(tie(in_hbm(grad), *token)[0], (), (0, 1), j, 0))
+        token = tuple(current[j])
 
     def after(array):
         return tie(array, *token)[0]
+
+    def moved(both, steps):
+        parts = []
+        for d in range(2):
+            parts.append(lax.ppermute(both[d], "dev", ahead(d, steps)))
+        return jnp.stack(parts)
+
+    places = after(chosen).reshape(pods, blocks, count, LANES)
+    own_places = lax.dynamic_index_in_dim(places, pod, 0, keepdims=False)
+    near = [moved(own_places, -steps) for steps in range(1, HOPS + 1)]
 
     def terms(s, j):
         source = after(grad)
@@ -311,69 +406,55 @@
         )
         return own[j]
 
-    def near_filler(j):
-        raw[j] = term_part(terms(last, j), after(spans(near, j)), wide_t, tall, members=members, **how)
+    def raw_filler(j):
+        others = [t for steps in range(1, HOPS) for t in terms(members - 1 - steps, j)]
+        where = jnp.concatenate([spans(p, j) for p in near[: HOPS - 1]], axis=0)
+        raw[j] = term_part(others, after(where), wide_t, tall, members=members, **how)
         return (raw[j],)
+
+    def sent_filler(j):
+        sent[j] = term_part(current[j], after(spans(near[-1], j)), wide_t, tall, members=members, **how)
+        return (sent[j],)
 
     def table_filler(j):
         tables[j] = table_part(after(spans(places, j)), tall, **how)
         return tables[j]
 
-    def far_filler(j):
-        sent[j] = term_part(current[j], after(spans(far, j)), wide_t, tall, members=members, **how)
-        return (sent[j],)
-
-    def moved(both, steps):
-        parts = []
-        for d in range(2):
-            parts.append(lax.ppermute(both[d], "dev", ahead(d, steps)))
-        return jnp.stack(parts)
-
     own, raw, tables, sent = ([None] * chunks for _ in range(4))
     arrivals = [[None] * 2 for _ in range(chunks)]
-    fillers = {
-        (0, 1): (own_filler, 0),
-        (1, 0): (own_filler, 1),
-        (1, 1): (near_filler, 0),
-        (2, 0): (near_filler, 1),
-        (2, 1): (table_filler, 0),
-        (3, 0): (table_filler, 1),
-        (cut - 1, 0): (far_filler, 0),
-        (cut - 1, 1): (far_filler, 1),
-    }
+    fillers = {send - 3: raw_filler, send - 2: own_filler, send - 1: sent_filler, send: table_filler}
     for s in range(members - 1):
         for j in range(chunks):
             for d in range(2):
                 arrived = lax.ppermute(current[j][d], "dev", ahead(d, 1))
                 if s < last:
                     arrived, source, *_ = tie(arrived, grad, *token)
-                    current[j][d] = arrived + piece(source, d, s + 1, j).astype(f32)
+                    if s == 0:
+                        (current[j][d],) = load(in_hbm(source), (arrived,), (d,), j, s + 1)
+                    else:
+                        current[j][d] = arrived + piece(source, d, s + 1, j).astype(f32)
                     token = (current[j][d],)
                 else:
                     arrivals[j][d] = arrived
-            if (s, j) == (0, 0):
-                places = after(chosen).reshape(pods, blocks, count, LANES)
-                own_places = lax.dynamic_index_in_dim(places, pod, 0, keepdims=False)
-                near = moved(own_places, -1)
-                far = moved(own_places, -2)
-            if (s, j) in fillers:
-                fill, i = fillers[s, j]
-                token += tuple(fill(i))
-            if (s, j) == (2, 0):
-                from_near = moved(jnp.concatenate(raw, axis=1), 1)
-            if (s, j) == (cut - 1, 1):
-                from_far = moved(jnp.concatenate(sent, axis=1), 2)
-            if (s, j) == (cut, 1):
-                values = jnp.concatenate([v for _, v in own], axis=1) + from_near + from_far
+            if s in fillers:
+                token += tuple(fillers[s](j))
+            if (s, j) == (send - 3, chunks - 1):
+                both = jnp.concatenate(raw, axis=1)
+                received = [moved(both[2 * n - 2 : 2 * n], n) for n in range(1, HOPS)]
+            if (s, j) == (send - 1, chunks - 1):
+                received.append(moved(jnp.concatenate(sent, axis=1), HOPS))
+            if (s, j) == (send + 1, 0):
+                values = jnp.concatenate([v for _, v in own], axis=1) + sum(received)
                 every = lax.all_gather(after(values), "outer")
                 token += (every,)
-    updates, outs = [], []
+    update, rests = None, []
     for j in range(chunks):
-        update, rest = decode_part(pod[None], after(spans(every, j)), *tables[j], own[j][0], wide, same, side)
-        token = (update,)
-        updates.append(update)
-        outs.append(rest + jnp.concatenate(arrivals[j], axis=0) / members)
-    return jnp.concatenate(outs, axis=1)[None], jnp.concatenate(updates, axis=1)
+        update, rest = decode_part(pod[None], after(every), tables[j], own[j][0], wide, same, side, j, chunks, update)
+        rests.append(rest)
+    out = None
+    for j in range(chunks):
+        out = finish_part(out, width, rests[j], arrivals[j], members, j * piece_cols)
+    return out[None], update
 
 
 def solution(mesh):

time: 124 us -> 136 us (1.097)
  other arithmetic: 14.2 us -> 0.76 us
  Pallas kernels: 12.3 us -> 23.9 us
  waiting for transfers between devices: 47.3 us -> 57.5 us
  starting transfers between devices: 41.4 us -> 46.4 us
  local copies, waits for them, and re-layouts: 2.29 us -> 0.45 us
    pallas_call x2 -> x10, Pallas kernels: 3.32 us -> 13 us  [the longest x6 6.11 us: load_part(): pl.pallas_call(functools.partial(load_kernel, members, side, j, s, ways),...]
    ppermute x8 -> x12, starting transfers between devices: 9.73 us -> 17.9 us  [moved(): parts.append(lax.ppermute(both[d], 'dev', ahead(d, steps)))]
    add x24 -> x20, other arithmetic: 6.23 us -> 0.7 us  [local(): current[j][d] = arrived + piece(source, d, s + 1, j).astype(f32)]
    convert_element_type x4 -> x0, other arithmetic: 5.33 us -> none  [local(): current[j][d] = piece(source, d, 0, j).astype(f32)]
    ppermute x8 -> x12, waiting for transfers between devices: 1.12 us -> 6.37 us  [moved(): parts.append(lax.ppermute(both[d], 'dev', ahead(d, steps)))]
    ppermute x28, waiting for transfers between devices: 46.2 us -> 51.2 us  [local(): arrived = lax.ppermute(current[j][d], 'dev', ahead(d, 1))]
    ppermute x28, starting transfers between devices: 31.6 us -> 28.5 us  [local(): arrived = lax.ppermute(current[j][d], 'dev', ahead(d, 1))]
    pallas_call x4, Pallas kernels: 4.77 us -> 6.66 us  [term_part(): pl.pallas_call(functools.partial(term_kernel, kept, side, members), out_s...]
  transfers between devices with their start and end apart: 36 -> 40, of which waited for: 15 -> 17; matrix products, arithmetic and copies ran while one was open for 11% -> 1% of each run, Pallas kernels for 10% -> 16%
where the time goes in v2:
time: 136 us
  waiting for transfers between devices  57.5 us (42%)
  starting transfers between devices  46.4 us (34%)
  Pallas kernels  23.9 us (18%)
  blocking collectives  5.22 us (4%)
    ppermute x28, waiting for transfers between devices, local(): arrived = lax.ppermute(current[j][d], 'dev', ahead(d, 1))  51.2 us
    ppermute x28, starting transfers between devices, local(): arrived = lax.ppermute(current[j][d], 'dev', ahead(d, 1))  28.5 us
    ppermute x12, starting transfers between devices, moved(): parts.append(lax.ppermute(both[d], 'dev', ahead(d, steps)))  17.9 us
    pallas_call x4, Pallas kernels, term_part(): pl.pallas_call(functools.partial(term_kernel, kept, side, members), out_s...  6.66 us
    ppermute x12, waiting for transfers between devices, moved(): parts.append(lax.ppermute(both[d], 'dev', ahead(d, steps)))  6.37 us
    pallas_call x6, Pallas kernels, load_part(): pl.pallas_call(functools.partial(load_kernel, members, side, j, s, ways),...  6.11 us
    all_gather x1, blocking collectives, local(): every = lax.all_gather(after(values), 'outer')  5.22 us
    pallas_call x2, Pallas kernels, decode_part(): pl.pallas_call(functools.partial(decode_kernel, side, chunk), out_shape=(...  5.11 us
  transfers between devices with their start and end apart: 40, of which 17 were waited for; matrix products, arithmetic and copies ran while one was open for 1% of the time, Pallas kernels for 16%

profile of v2, /device:TPU:0, one launch (start us, length us, event | category | flops | bytes accessed | tf_op | source)
XLA Modules:
  0.0 135.5 jit_solution(3009510533106598165)
XLA Ops:
  1.7 3.0 %collective-permute-start = (f32[64,1280]{1,0:T(8,128)S(1)}, f32[64,1280]{1,0:T(8,128)S(1)}, u32[]{:S(2)}, u32[]{:S(2)}) collective-permute-start(f32[64,1280]{1,0:T(8,128)S(1)} %get-tuple-element.82), channel_id=1, source_target_pairs={{0,1},{2,0},{4,2},{6,4},{7,6},{5,7},{3,5},{1,3},{8,9},{10,8},{12,1... | collective-permute-start | bytes 983048 | tf_op jit(solution)/shard_map/ppermute | solution.py:429
  6.2 4.0 %collective-permute-start.23 = (s32[10,128]{1,0:T(8,128)S(1)}, s32[10,128]{1,0:T(8,128)S(1)}, u32[]{:S(2)}, u32[]{:S(2)}) collective-permute-start(s32[10,128]{1,0:T(8,128)S(1)} %get-tuple-element.176), channel_id=1, source_target_pairs={{0,6},{2,7},{4,5},{6,3},{7,1},{5,0},{3,2},{1,4},{8,14},{10,15},{12... | collective-permute-start | bytes 15368 | tf_op jit(solution)/shard_map/ppermute | solution.py:385
  10.7 2.3 %collective-permute-start.22 = (s32[10,128]{1,0:T(8,128)S(1)}, s32[10,128]{1,0:T(8,128)S(1)}, u32[]{:S(2)}, u32[]{:S(2)}) collective-permute-start(s32[10,128]{1,0:T(8,128)S(1)} %get-tuple-element.177), channel_id=1, source_target_pairs={{0,5},{2,3},{4,1},{6,0},{7,2},{5,4},{3,6},{1,7},{8,13},{10,11},{12... | collective-permute-start | bytes 15368 | tf_op jit(solution)/shard_map/ppermute | solution.py:385
  13.0 3.4 %collective-permute-done.23 = s32[10,128]{1,0:T(8,128)S(1)} collective-permute-done((s32[10,128]{1,0:T(8,128)S(1)}, s32[10,128]{1,0:T(8,128)S(1)}, u32[]{:S(2)}, u32[]{:S(2)}) %collective-permute-start.23) | collective-permute-done | bytes 5152 | tf_op jit(solution)/shard_map/ppermute | solution.py:385
  16.5 2.9 %collective-permute-start.12 = (s32[10,128]{1,0:T(8,128)S(1)}, s32[10,128]{1,0:T(8,128)S(1)}, u32[]{:S(2)}, u32[]{:S(2)}) collective-permute-start(s32[10,128]{1,0:T(8,128)S(1)} %get-tuple-element.177), channel_id=1, source_target_pairs={{0,3},{2,1},{4,0},{6,2},{7,4},{5,6},{3,7},{1,5},{8,11},{10,9},{12,... | collective-permute-start | bytes 15368 | tf_op jit(solution)/shard_map/ppermute | solution.py:385
  20.5 2.0 %collective-permute-start.5 = (f32[64,1280]{1,0:T(8,128)S(1)}, f32[64,1280]{1,0:T(8,128)S(1)}, u32[]{:S(2)}, u32[]{:S(2)}) collective-permute-start(f32[64,1280]{1,0:T(8,128)S(1)} %get-tuple-element.85), channel_id=1, source_target_pairs={{0,2},{2,4},{4,6},{6,7},{7,5},{5,3},{3,1},{1,0},{8,10},{10,12},{12... | collective-permute-start | bytes 983048 | tf_op jit(solution)/shard_map/ppermute | solution.py:429
  22.6 2.0 %collective-permute-start.3 = (f32[64,1280]{1,0:T(8,128)S(1)}, f32[64,1280]{1,0:T(8,128)S(1)}, u32[]{:S(2)}, u32[]{:S(2)}) collective-permute-start(f32[64,1280]{1,0:T(8,128)S(1)} %shard_map.88), channel_id=1, source_target_pairs={{0,2},{2,4},{4,6},{6,7},{7,5},{5,3},{3,1},{1,0},{8,10},{10,12},{12... | collective-permute-start | bytes 983048 | tf_op jit(solution)/shard_map/ppermute | solution.py:429
  25.9 5.2 %collective-permute-done.5.refs_0_ = f32[64,1280]{1,0:T(8,128)S(1)} collective-permute-done((f32[64,1280]{1,0:T(8,128)S(1)}, f32[64,1280]{1,0:T(8,128)S(1)}, u32[]{:S(2)}, u32[]{:S(2)}) %collective-permute-start.5) | collective-permute-done | bytes 327712 | tf_op jit(solution)/shard_map/ppermute | solution.py:429
  32.1 2.0 %collective-permute-start.9 = (f32[64,1280]{1,0:T(8,128)S(1)}, f32[64,1280]{1,0:T(8,128)S(1)}, u32[]{:S(2)}, u32[]{:S(2)}) collective-permute-start(f32[64,1280]{1,0:T(8,128)S(1)} %shard_map.90), channel_id=1, source_target_pairs={{0,2},{2,4},{4,6},{6,7},{7,5},{5,3},{3,1},{1,0},{8,10},{10,12},{12... | collective-permute-start | bytes 983048 | tf_op jit(solution)/shard_map/ppermute | solution.py:429
  35.2 2.9 %collective-permute-done.3 = f32[64,1280]{1,0:T(8,128)S(1)} collective-permute-done((f32[64,1280]{1,0:T(8,128)S(1)}, f32[64,1280]{1,0:T(8,128)S(1)}, u32[]{:S(2)}, u32[]{:S(2)}) %collective-permute-start.3) | collective-permute-done | bytes 327712 | tf_op jit(solution)/shard_map/ppermute | solution.py:429
  40.3 2.0 %collective-permute-start.7 = (f32[64,1280]{1,0:T(8,128)S(1)}, f32[64,1280]{1,0:T(8,128)S(1)}, u32[]{:S(2)}, u32[]{:S(2)}) collective-permute-start(f32[64,1280]{1,0:T(8,128)S(1)} %convert_add_fusion.19), channel_id=1, source_target_pairs={{0,2},{2,4},{4,6},{6,7},{7,5},{5,3},{3,1},{1,0},{8,10},{10,12},{12... | collective-permute-start | bytes 983048 | tf_op jit(solution)/shard_map/ppermute | solution.py:429
  42.3 2.1 %shard_map.92 = f32[4,5,128]{2,1,0:T(8,128)S(1)} custom-call(bf16[64,1280]{1,0:T(8,128)(2,1)S(1)} %get-tuple-element.173.refs_0_, bf16[64,1280]{1,0:T(8,128)(2,1)S(1)} %get-tuple-element.172.refs_1_, bf16[64,1280]{1,0:T(8,128)(2,1)S(1)} %get-tuple-element.171.refs_2_, bf16[64,1280]{1,0:T(8,128)(2,1)S(1)} %get-tuple-element.170.refs_3_, ...), custom_call_target="tpu_custom_call" | custom-call | flops 1677721600 | bytes 655360 | tf_op jit(solution)/shard_map/pallas_call | solution.py:140
  47.3 2.0 %collective-permute-start.15 = (f32[64,1280]{1,0:T(8,128)S(1)}, f32[64,1280]{1,0:T(8,128)S(1)}, u32[]{:S(2)}, u32[]{:S(2)}) collective-permute-start(f32[64,1280]{1,0:T(8,128)S(1)} %convert_add_fusion.17), channel_id=1, source_target_pairs={{0,2},{2,4},{4,6},{6,7},{7,5},{5,3},{3,1},{1,0},{8,10},{10,12},{12... | collective-permute-start | bytes 983048 | tf_op jit(solution)/shard_map/ppermute | solution.py:429
  49.3 2.1 %shard_map.93 = f32[4,5,128]{2,1,0:T(8,128)S(1)} custom-call(bf16[64,1280]{1,0:T(8,128)(2,1)S(1)} %get-tuple-element.169.refs_0_, bf16[64,1280]{1,0:T(8,128)(2,1)S(1)} %get-tuple-element.168.refs_1_, bf16[64,1280]{1,0:T(8,128)(2,1)S(1)} %get-tuple-element.167.refs_2_, bf16[64,1280]{1,0:T(8,128)(2,1)S(1)} %get-tuple-element.166.refs_3_, ...), custom_call_target="tpu_custom_call" | custom-call | flops 1677721600 | bytes 655360 | tf_op jit(solution)/shard_map/pallas_call | solution.py:140
  60.0 5.1 %collective-permute-done.20 = f32[64,1280]{1,0:T(8,128)S(1)} collective-permute-done((f32[64,1280]{1,0:T(8,128)S(1)}, f32[64,1280]{1,0:T(8,128)S(1)}, u32[]{:S(2)}, u32[]{:S(2)}) %collective-permute-start.20) | collective-permute-done | bytes 327712 | tf_op jit(solution)/shard_map/ppermute | solution.py:429
  65.4 6.8 %collective-permute-done.21 = f32[64,1280]{1,0:T(8,128)S(1)} collective-permute-done((f32[64,1280]{1,0:T(8,128)S(1)}, f32[64,1280]{1,0:T(8,128)S(1)}, u32[]{:S(2)}, u32[]{:S(2)}) %collective-permute-start.21) | collective-permute-done | bytes 327712 | tf_op jit(solution)/shard_map/ppermute | solution.py:429
  74.1 5.2 %collective-permute-done.24 = f32[64,1280]{1,0:T(8,128)S(1)} collective-permute-done((f32[64,1280]{1,0:T(8,128)S(1)}, f32[64,1280]{1,0:T(8,128)S(1)}, u32[]{:S(2)}, u32[]{:S(2)}) %collective-permute-start.24) | collective-permute-done | bytes 327712 | tf_op jit(solution)/shard_map/ppermute | solution.py:429
  79.5 6.9 %collective-permute-done.25 = f32[64,1280]{1,0:T(8,128)S(1)} collective-permute-done((f32[64,1280]{1,0:T(8,128)S(1)}, f32[64,1280]{1,0:T(8,128)S(1)}, u32[]{:S(2)}, u32[]{:S(2)}) %collective-permute-start.25) | collective-permute-done | bytes 327712 | tf_op jit(solution)/shard_map/ppermute | solution.py:429
  88.7 3.3 %collective-permute-start.26 = (f32[10,128]{1,0:T(8,128)S(1)}, f32[10,128]{1,0:T(8,128)S(1)}, u32[]{:S(2)}, u32[]{:S(2)}) collective-permute-start(f32[10,128]{1,0:T(8,128)S(1)} %get-tuple-element.182), channel_id=1, source_target_pairs={{0,6},{2,7},{4,5},{6,3},{7,1},{5,0},{3,2},{1,4},{8,14},{10,15},{12... | collective-permute-start | bytes 15368 | tf_op jit(solution)/shard_map/ppermute | solution.py:385
  94.7 2.9 %collective-permute-done.26 = f32[10,128]{1,0:T(8,128)S(1)} collective-permute-done((f32[10,128]{1,0:T(8,128)S(1)}, f32[10,128]{1,0:T(8,128)S(1)}, u32[]{:S(2)}, u32[]{:S(2)}) %collective-permute-start.26) | collective-permute-done | bytes 5152 | tf_op jit(solution)/shard_map/ppermute | solution.py:385
  99.7 10.5 %collective-permute-done.28 = f32[64,1280]{1,0:T(8,128)S(1)} collective-permute-done((f32[64,1280]{1,0:T(8,128)S(1)}, f32[64,1280]{1,0:T(8,128)S(1)}, u32[]{:S(2)}, u32[]{:S(2)}) %collective-permute-start.28) | collective-permute-done | bytes 327712 | tf_op jit(solution)/shard_map/ppermute | solution.py:429
  119.1 5.2 %all-gather = f32[8,10,128]{2,1,0:T(8,128)S(1)} all-gather(f32[2,10,128]{2,1,0:T(8,128)S(1)} %maximum_add_fusion), channel_id=2, replica_groups=mesh['outer'=4,'dev'=8] {'outer'}, dimensions={0}, use_global_device_ids=true | all-gather | bytes 51200 | tf_op jit(solution)/shard_map/all_gather | solution.py:448
  126.5 2.5 %shard_map.100 = (f32[128,2560]{1,0:T(8,128)}, f32[128,1280]{1,0:T(8,128)S(1)}) custom-call(s32[1]{0:T(128)} %bitcast.pod_ref, f32[4,2,10,128]{3,2,1,0:T(8,128)S(1)} %bitcast.39, f32[2,5,64,512]{3,2,1,0:T(8,128)S(1)} %get-tuple-element.139.rows_ref, bf16[2,5,512,256]{3,2,1,0:T(8,128)(2,1)S(1)} %get-tuple-element.140.cols_ref, ...), custom_call_target="tpu_custom_call" | custom-call | flops 838860800 | bytes 1966080 | tf_op jit(solution)/shard_map/pallas_call | solution.py:220
  129.0 2.6 %shard_map.101 = (f32[128,2560]{1,0:T(8,128)}, f32[128,1280]{1,0:T(8,128)S(1)}) custom-call(s32[1]{0:T(128)} %bitcast.pod_ref, f32[4,2,10,128]{3,2,1,0:T(8,128)S(1)} %bitcast.40, f32[2,5,64,512]{3,2,1,0:T(8,128)S(1)} %get-tuple-element.146.rows_ref, bf16[2,5,512,256]{3,2,1,0:T(8,128)(2,1)S(1)} %get-tuple-element.147.cols_ref, ...), custom_call_target="tpu_custom_call", output_to_operand_aliasing={{0}: (7, {})} | custom-call | flops 838860800 | bytes 1966080 | tf_op jit(solution)/shard_map/pallas_call | solution.py:220
  (129 shorter events, 44.8 us)
Async XLA Ops:
  1.7 22.9 %collective-permute-start = (f32[64,1280]{1,0:T(8,128)S(1)}, f32[64,1280]{1,0:T(8,128)S(1)}, u32[]{:S(2)}, u32[]{:S(2)}) collective-permute-start(f32[64,1280]{1,0:T(8,128)S(1)} %get-tuple-element.82), channel_id=1, source_target_pairs={{0,1},{2,0},{4,2},{6,4},{7,6},{5,7},{3,5},{1,3},{8,9},{10,8},{12,1... | collective-permute-start | bytes 983048 | tf_op jit(solution)/shard_map/ppermute | solution.py:429
  4.8 14.7 %collective-permute-start.1 = (f32[64,1280]{1,0:T(8,128)S(1)}, f32[64,1280]{1,0:T(8,128)S(1)}, u32[]{:S(2)}, u32[]{:S(2)}) collective-permute-start(f32[64,1280]{1,0:T(8,128)S(1)} %get-tuple-element.83), channel_id=1, source_target_pairs={{0,2},{2,4},{4,6},{6,7},{7,5},{5,3},{3,1},{1,0},{8,10},{10,12},{12... | collective-permute-start | bytes 983048 | tf_op jit(solution)/shard_map/ppermute | solution.py:429
  20.5 10.6 %collective-permute-start.5 = (f32[64,1280]{1,0:T(8,128)S(1)}, f32[64,1280]{1,0:T(8,128)S(1)}, u32[]{:S(2)}, u32[]{:S(2)}) collective-permute-start(f32[64,1280]{1,0:T(8,128)S(1)} %get-tuple-element.85), channel_id=1, source_target_pairs={{0,2},{2,4},{4,6},{6,7},{7,5},{5,3},{3,1},{1,0},{8,10},{10,12},{12... | collective-permute-start | bytes 983048 | tf_op jit(solution)/shard_map/ppermute | solution.py:429
  22.5 11.6 %collective-permute-start.4 = (f32[64,1280]{1,0:T(8,128)S(1)}, f32[64,1280]{1,0:T(8,128)S(1)}, u32[]{:S(2)}, u32[]{:S(2)}) collective-permute-start(f32[64,1280]{1,0:T(8,128)S(1)} %get-tuple-element.86), channel_id=1, source_target_pairs={{0,1},{2,0},{4,2},{6,4},{7,6},{5,7},{3,5},{1,3},{8,9},{10,8},{12,1... | collective-permute-start | bytes 983048 | tf_op jit(solution)/shard_map/ppermute | solution.py:429
  22.6 15.6 %collective-permute-start.3 = (f32[64,1280]{1,0:T(8,128)S(1)}, f32[64,1280]{1,0:T(8,128)S(1)}, u32[]{:S(2)}, u32[]{:S(2)}) collective-permute-start(f32[64,1280]{1,0:T(8,128)S(1)} %shard_map.88), channel_id=1, source_target_pairs={{0,2},{2,4},{4,6},{6,7},{7,5},{5,3},{3,1},{1,0},{8,10},{10,12},{12... | collective-permute-start | bytes 983048 | tf_op jit(solution)/shard_map/ppermute | solution.py:429
  25.8 14.4 %collective-permute-start.2 = (f32[64,1280]{1,0:T(8,128)S(1)}, f32[64,1280]{1,0:T(8,128)S(1)}, u32[]{:S(2)}, u32[]{:S(2)}) collective-permute-start(f32[64,1280]{1,0:T(8,128)S(1)} %shard_map.89), channel_id=1, source_target_pairs={{0,1},{2,0},{4,2},{6,4},{7,6},{5,7},{3,5},{1,3},{8,9},{10,8},{12,1... | collective-permute-start | bytes 983048 | tf_op jit(solution)/shard_map/ppermute | solution.py:429
  32.1 13.1 %collective-permute-start.9 = (f32[64,1280]{1,0:T(8,128)S(1)}, f32[64,1280]{1,0:T(8,128)S(1)}, u32[]{:S(2)}, u32[]{:S(2)}) collective-permute-start(f32[64,1280]{1,0:T(8,128)S(1)} %shard_map.90), channel_id=1, source_target_pairs={{0,2},{2,4},{4,6},{6,7},{7,5},{5,3},{3,1},{1,0},{8,10},{10,12},{12... | collective-permute-start | bytes 983048 | tf_op jit(solution)/shard_map/ppermute | solution.py:429
  35.1 12.0 %collective-permute-start.8 = (f32[64,1280]{1,0:T(8,128)S(1)}, f32[64,1280]{1,0:T(8,128)S(1)}, u32[]{:S(2)}, u32[]{:S(2)}) collective-permute-start(f32[64,1280]{1,0:T(8,128)S(1)} %shard_map.91), channel_id=1, source_target_pairs={{0,1},{2,0},{4,2},{6,4},{7,6},{5,7},{3,5},{1,3},{8,9},{10,8},{12,1... | collective-permute-start | bytes 983048 | tf_op jit(solution)/shard_map/ppermute | solution.py:429
  40.2 14.0 %collective-permute-start.6 = (f32[64,1280]{1,0:T(8,128)S(1)}, f32[64,1280]{1,0:T(8,128)S(1)}, u32[]{:S(2)}, u32[]{:S(2)}) collective-permute-start(f32[64,1280]{1,0:T(8,128)S(1)} %convert_add_fusion.18), channel_id=1, source_target_pairs={{0,1},{2,0},{4,2},{6,4},{7,6},{5,7},{3,5},{1,3},{8,9},{10,8},{12,1... | collective-permute-start | bytes 983048 | tf_op jit(solution)/shard_map/ppermute | solution.py:429
  40.3 11.9 %collective-permute-start.7 = (f32[64,1280]{1,0:T(8,128)S(1)}, f32[64,1280]{1,0:T(8,128)S(1)}, u32[]{:S(2)}, u32[]{:S(2)}) collective-permute-start(f32[64,1280]{1,0:T(8,128)S(1)} %convert_add_fusion.19), channel_id=1, source_target_pairs={{0,2},{2,4},{4,6},{6,7},{7,5},{5,3},{3,1},{1,0},{8,10},{10,12},{12... | collective-permute-start | bytes 983048 | tf_op jit(solution)/shard_map/ppermute | solution.py:429
  47.2 10.8 %collective-permute-start.14 = (f32[64,1280]{1,0:T(8,128)S(1)}, f32[64,1280]{1,0:T(8,128)S(1)}, u32[]{:S(2)}, u32[]{:S(2)}) collective-permute-start(f32[64,1280]{1,0:T(8,128)S(1)} %convert_add_fusion.16), channel_id=1, source_target_pairs={{0,1},{2,0},{4,2},{6,4},{7,6},{5,7},{3,5},{1,3},{8,9},{10,8},{12,1... | collective-permute-start | bytes 983048 | tf_op jit(solution)/shard_map/ppermute | solution.py:429
  51.5 37.2 %collective-permute-start.18 = (f32[10,128]{1,0:T(8,128)S(1)}, f32[10,128]{1,0:T(8,128)S(1)}, u32[]{:S(2)}, u32[]{:S(2)}) collective-permute-start(f32[10,128]{1,0:T(8,128)S(1)} %get-tuple-element.178), channel_id=1, source_target_pairs={{0,4},{2,6},{4,7},{6,5},{7,3},{5,1},{3,0},{1,2},{8,12},{10,14},{12... | collective-permute-start | bytes 15368 | tf_op jit(solution)/shard_map/ppermute | solution.py:385
  52.2 39.8 %collective-permute-start.16 = (f32[10,128]{1,0:T(8,128)S(1)}, f32[10,128]{1,0:T(8,128)S(1)}, u32[]{:S(2)}, u32[]{:S(2)}) collective-permute-start(f32[10,128]{1,0:T(8,128)S(1)} %get-tuple-element.179), channel_id=1, source_target_pairs={{0,2},{2,4},{4,6},{6,7},{7,5},{5,3},{3,1},{1,0},{8,10},{10,12},{12... | collective-permute-start | bytes 15368 | tf_op jit(solution)/shard_map/ppermute | solution.py:385
  54.2 38.3 %collective-permute-start.17 = (f32[10,128]{1,0:T(8,128)S(1)}, f32[10,128]{1,0:T(8,128)S(1)}, u32[]{:S(2)}, u32[]{:S(2)}) collective-permute-start(f32[10,128]{1,0:T(8,128)S(1)} %get-tuple-element.180), channel_id=1, source_target_pairs={{0,1},{2,0},{4,2},{6,4},{7,6},{5,7},{3,5},{1,3},{8,9},{10,8},{12,1... | collective-permute-start | bytes 15368 | tf_op jit(solution)/shard_map/ppermute | solution.py:385
  56.1 38.1 %collective-permute-start.19 = (f32[10,128]{1,0:T(8,128)S(1)}, f32[10,128]{1,0:T(8,128)S(1)}, u32[]{:S(2)}, u32[]{:S(2)}) collective-permute-start(f32[10,128]{1,0:T(8,128)S(1)} %get-tuple-element.181), channel_id=1, source_target_pairs={{0,3},{2,1},{4,0},{6,2},{7,4},{5,6},{3,7},{1,5},{8,11},{10,9},{12,... | collective-permute-start | bytes 15368 | tf_op jit(solution)/shard_map/ppermute | solution.py:385
  86.4 12.6 %collective-permute-start.29 = (f32[64,1280]{1,0:T(8,128)S(1)}, f32[64,1280]{1,0:T(8,128)S(1)}, u32[]{:S(2)}, u32[]{:S(2)}) collective-permute-start(f32[64,1280]{1,0:T(8,128)S(1)} %convert_add_fusion.11.refs_0_), channel_id=1, source_target_pairs={{0,2},{2,4},{4,6},{6,7},{7,5},{5,3},{3,1},{1,0},{8,10},{10,12},{12... | collective-permute-start | bytes 983048 | tf_op jit(solution)/shard_map/ppermute | solution.py:429
  92.6 21.3 %collective-permute-start.32 = (f32[64,1280]{1,0:T(8,128)S(1)}, f32[64,1280]{1,0:T(8,128)S(1)}, u32[]{:S(2)}, u32[]{:S(2)}) collective-permute-start(f32[64,1280]{1,0:T(8,128)S(1)} %convert_add_fusion.8.refs_1_), channel_id=1, source_target_pairs={{0,1},{2,0},{4,2},{6,4},{7,6},{5,7},{3,5},{1,3},{8,9},{10,8},{12,1... | collective-permute-start | bytes 983048 | tf_op jit(solution)/shard_map/ppermute | solution.py:429
  94.1 18.7 %collective-permute-start.33 = (f32[64,1280]{1,0:T(8,128)S(1)}, f32[64,1280]{1,0:T(8,128)S(1)}, u32[]{:S(2)}, u32[]{:S(2)}) collective-permute-start(f32[64,1280]{1,0:T(8,128)S(1)} %convert_add_fusion.9.refs_0_), channel_id=1, source_target_pairs={{0,2},{2,4},{4,6},{6,7},{7,5},{5,3},{3,1},{1,0},{8,10},{10,12},{12... | collective-permute-start | bytes 983048 | tf_op jit(solution)/shard_map/ppermute | solution.py:429
  97.6 12.6 %collective-permute-start.28 = (f32[64,1280]{1,0:T(8,128)S(1)}, f32[64,1280]{1,0:T(8,128)S(1)}, u32[]{:S(2)}, u32[]{:S(2)}) collective-permute-start(f32[64,1280]{1,0:T(8,128)S(1)} %convert_add_fusion.10.refs_1_), channel_id=1, source_target_pairs={{0,1},{2,0},{4,2},{6,4},{7,6},{5,7},{3,5},{1,3},{8,9},{10,8},{12,1... | collective-permute-start | bytes 983048 | tf_op jit(solution)/shard_map/ppermute | solution.py:429
  99.1 16.9 %collective-permute-start.31 = (f32[64,1280]{1,0:T(8,128)S(1)}, f32[64,1280]{1,0:T(8,128)S(1)}, u32[]{:S(2)}, u32[]{:S(2)}) collective-permute-start(f32[64,1280]{1,0:T(8,128)S(1)} %convert_add_fusion.7), channel_id=1, source_target_pairs={{0,2},{2,4},{4,6},{6,7},{7,5},{5,3},{3,1},{1,0},{8,10},{10,12},{12... | collective-permute-start | bytes 983048 | tf_op jit(solution)/shard_map/ppermute | solution.py:429
  112.9 11.4 %collective-permute-start.35 = (f32[64,1280]{1,0:T(8,128)S(1)}, f32[64,1280]{1,0:T(8,128)S(1)}, u32[]{:S(2)}, u32[]{:S(2)}) collective-permute-start(f32[64,1280]{1,0:T(8,128)S(1)} %convert_add_fusion.5), channel_id=1, source_target_pairs={{0,2},{2,4},{4,6},{6,7},{7,5},{5,3},{3,1},{1,0},{8,10},{10,12},{12... | collective-permute-start | bytes 983048 | tf_op jit(solution)/shard_map/ppermute | solution.py:429
  113.9 10.5 %collective-permute-start.34 = (f32[64,1280]{1,0:T(8,128)S(1)}, f32[64,1280]{1,0:T(8,128)S(1)}, u32[]{:S(2)}, u32[]{:S(2)}) collective-permute-start(f32[64,1280]{1,0:T(8,128)S(1)} %convert_add_fusion.4), channel_id=1, source_target_pairs={{0,1},{2,0},{4,2},{6,4},{7,6},{5,7},{3,5},{1,3},{8,9},{10,8},{12,1... | collective-permute-start | bytes 983048 | tf_op jit(solution)/shard_map/ppermute | solution.py:429
  116.0 15.6 %collective-permute-start.38 = (f32[64,1280]{1,0:T(8,128)S(1)}, f32[64,1280]{1,0:T(8,128)S(1)}, u32[]{:S(2)}, u32[]{:S(2)}) collective-permute-start(f32[64,1280]{1,0:T(8,128)S(1)} %convert_add_fusion.3), channel_id=1, source_target_pairs={{0,2},{2,4},{4,6},{6,7},{7,5},{5,3},{3,1},{1,0},{8,10},{10,12},{12... | collective-permute-start | bytes 983048 | tf_op jit(solution)/shard_map/ppermute | solution.py:429
  117.9 13.7 %collective-permute-start.39 = (f32[64,1280]{1,0:T(8,128)S(1)}, f32[64,1280]{1,0:T(8,128)S(1)}, u32[]{:S(2)}, u32[]{:S(2)}) collective-permute-start(f32[64,1280]{1,0:T(8,128)S(1)} %convert_add_fusion.2), channel_id=1, source_target_pairs={{0,1},{2,0},{4,2},{6,4},{7,6},{5,7},{3,5},{1,3},{8,9},{10,8},{12,1... | collective-permute-start | bytes 983048 | tf_op jit(solution)/shard_map/ppermute | solution.py:429
  (24 other events, 263.3 us)

commit v3 on v2

--- a/solution.py
+++ b/solution.py
@@ -28,23 +28,36 @@
     return (weight * np.cos(np.pi * (2.0 * place + 1.0) * freq / (2.0 * size))).astype(np.float32)
 
 
-def halves_of(table):
-    high = table.astype(bf16)
-    return np.stack([high, (table - high.astype(np.float32)).astype(bf16)])
-
-
-def split(x):
-    high = x.astype(bf16)
-    return high, (x - high.astype(f32)).astype(bf16)
+def parts_of(table):
+    parts = []
+    for _ in range(3):
+        parts.append(table.astype(bf16))
+        table = table - parts[-1].astype(np.float32)
+    return np.stack(parts)
+
+
+def split(x, count=3):
+    parts = []
+    for _ in range(count):
+        parts.append(x.astype(bf16))
+        x = x - parts[-1].astype(f32)
+    return parts
 
 
 def mm(a, b):
     return jnp.dot(a, b, preferred_element_type=f32)
 
 
-def mm3(x, table):
-    high, low = split(x)
-    return mm(high, table[0]) + (mm(low, table[0]) + mm(high, table[1]))
+def pick(x, one_hots, count=3):
+    return sum(mm(part, one_hots) for part in reversed(split(x, count)))
+
+
+def product(x, table):
+    if x.dtype == bf16:
+        return mm(x, table[0]) + (mm(x, table[1]) + mm(x, table[2]))
+    high, middle, low = split(x)
+    small = mm(low, table[0]) + (mm(middle, table[1]) + mm(high, table[2]))
+    return mm(high, table[0]) + (mm(middle, table[0]) + (mm(high, table[1]) + small))
 
 
 def log2(n):
@@ -64,17 +77,16 @@
 
 def basis_rows(row, tall, side):
     at_row = one_hot(lax.broadcasted_iota(jnp.int32, (side, row.shape[1]), 0) == row)
-    return mm(tall[0], at_row) + mm(tall[1], at_row)
+    return mm(tall[0], at_row) + (mm(tall[1], at_row) + mm(tall[2], at_row))
 
 
 def picks_of(xs, places, wide_t, tall, kept, side):
-    high, low = split(mm3(jnp.concatenate(xs, axis=0), wide_t))
+    spectra = product(jnp.concatenate(xs, axis=0), wide_t)
     found = []
     for i, idx in enumerate(places):
         row, col = table_places(idx, kept, side)
-        at_col = one_hot(lax.broadcasted_iota(jnp.int32, (high.shape[1], idx.shape[1]), 0) == col)
-        at = slice(i * side, (i + 1) * side)
-        cols = mm(high[at], at_col) + mm(low[at], at_col)
+        at_col = one_hot(lax.broadcasted_iota(jnp.int32, (spectra.shape[1], idx.shape[1]), 0) == col)
+        cols = pick(spectra[i * side : (i + 1) * side], at_col)
         found.append(jnp.sum(cols * basis_rows(row, tall, side), axis=0, keepdims=True))
     return found
 
@@ -107,9 +119,9 @@
         x += grad_refs[r][:, pl.ds(q * span, span)].astype(f32) / members
         x_ref[rows, pl.ds(q * span, span)] = x
         xs.append(x)
-    places = [idx_ref[r, pl.ds(q, 1), :] for r, q in spots]
+    places = [idx_ref[r, q] for r, q in spots]
     for (r, q), v in zip(spots, picks_of(xs, places, wide_t_ref, tall_ref, kept, side)):
-        v_ref[r, pl.ds(q, 1), :] = v
+        v_ref[r, q] = v
 
 
 def own_part(mom, terms, idx, wide_t, tall, kept, side, members, first):
@@ -130,10 +142,10 @@
     parts, count = idx_ref.shape[:2]
     span = wide_t_ref.shape[1]
     spots = [(r, q) for r in range(parts) for q in range(count)]
-    xs = [x_refs[r][:, pl.ds(q * span, span)].astype(f32) for r, q in spots]
-    places = [idx_ref[r, pl.ds(q, 1), :] for r, q in spots]
+    xs = [x_refs[r][:, pl.ds(q * span, span)] for r, q in spots]
+    places = [idx_ref[r, q] for r, q in spots]
     for (r, q), v in zip(spots, picks_of(xs, places, wide_t_ref, tall_ref, kept, side)):
-        v_ref[r, pl.ds(q, 1), :] = v / members
+        v_ref[r, q] = v / members
 
 
 def term_part(terms, idx, wide_t, tall, kept, side, members):
@@ -152,7 +164,7 @@
     span = cols_ref.shape[3]
     for r in range(parts):
         for q in range(count):
-            idx = jnp.concatenate([idx_ref[p, r, pl.ds(q, 1), :] for p in range(pods)], axis=1)
+            idx = jnp.concatenate([idx_ref[p, r, q] for p in range(pods)], axis=1)
             row, col = table_places(idx, kept, side)
             rows_ref[r, q] = basis_rows(row, tall_ref, side)
             tall_col = jnp.transpose(jnp.broadcast_to(col, (LANES, col.shape[1])))
@@ -162,7 +174,7 @@
 
 
 def table_part(idx, tall, kept, side):
-    pods, parts, count, lanes = idx.shape
+    pods, parts, count, _, lanes = idx.shape
     span = LANES // kept * side
     return pl.pallas_call(
         functools.partial(table_kernel, kept, side),
@@ -184,18 +196,15 @@
     mine = (lax.broadcasted_iota(jnp.int32, (1, lanes), 1) >> log2(LANES)) == pod_ref[0]
     for r in range(parts):
         for q in range(count):
-            at = pl.ds(chunk * count + q, 1)
-            v = jnp.concatenate([v_ref[p, r, at, :] for p in range(pods)], axis=1)
+            v = jnp.concatenate([v_ref[p, r, chunk * count + q] for p in range(pods)], axis=1)
             rows = rows_ref[r, q]
             sides = jnp.concatenate([rows * v, rows * jnp.where(mine, v, 0.0)], axis=0)
-            high, low = split(sides)
-            table_ref[r * count + q] = mm(high, cols_ref[r, q]) + mm(low, cols_ref[r, q])
+            table_ref[r * count + q] = pick(sides, cols_ref[r, q])
     table = table_ref[...].reshape(parts * count * 2 * side, span)
-    spatial = mm3(table, wide_ref).reshape(parts * count, 2, side, span)
+    spatial = product(table, wide_ref).reshape(parts * count, 2, side, span)
     shared = spatial[:, 0]
     squares = jnp.sum(shared * shared, axis=1) / (side * side)
-    high, low = split(squares)
-    mean = mm(high, same_ref[...]) + mm(low, same_ref[...])
+    mean = pick(squares, same_ref[...])
     scale = 1.0 / jnp.sqrt(mean + tiny_eps)
     for r in range(parts):
         for q in range(count):
@@ -324,7 +333,7 @@
 
     basis = cosine_basis(side)
     many = np.kron(np.eye(per, dtype=np.float32), basis)
-    wide, wide_t, tall = (jnp.asarray(halves_of(t)) for t in (many, many.T, basis.T))
+    wide, wide_t, tall = (jnp.asarray(parts_of(t)) for t in (many, many.T, basis.T))
     same = jnp.asarray(np.kron(np.eye(per), np.ones((side, side))).astype(bf16))
     how = dict(kept=kept, side=side)
 
@@ -335,7 +344,7 @@
         mom, summed = (jnp.pad(a, ((0, 0), (0, pad))) for a in (mom, summed))
         places = jnp.pad(chosen, ((0, 0), (0, 0), (0, pad // side), (0, 0)))
         count = (width + pad) // span
-        places = places.reshape(pods, blocks, count, LANES)
+        places = places.reshape(pods, blocks, count, 1, LANES)
         own_places = lax.dynamic_index_in_dim(places, pod, 0, keepdims=False)
         terms = [summed[r * side : (r + 1) * side] for r in range(blocks)]
         x, v = own_part(mom, terms, own_places, wide_t, tall, members=members, first=0, **how)
@@ -365,7 +374,7 @@
         return lax.optimization_barrier(arrays)
 
     def spans(a, j):
-        return a[..., j * each : (j + 1) * each, :]
+        return a[..., j * each : (j + 1) * each, :, :]
 
     last = members - 2
     send = last + 1 - HOPS
@@ -385,9 +394,12 @@
             parts.append(lax.ppermute(both[d], "dev", ahead(d, steps)))
         return jnp.stack(parts)
 
-    places = after(chosen).reshape(pods, blocks, count, LANES)
+    places = after(chosen).reshape(pods, blocks, count, 1, LANES)
     own_places = lax.dynamic_index_in_dim(places, pod, 0, keepdims=False)
-    near = [moved(own_places, -steps) for steps in range(1, HOPS + 1)]
+    near = [own_places]
+    for _ in range(1, HOPS + 1):
+        near.append(moved(near[-1], -1))
+    near = near[1:]
 
     def terms(s, j):
         source = after(grad)
@@ -422,7 +434,7 @@
 
     own, raw, tables, sent = ([None] * chunks for _ in range(4))
     arrivals = [[None] * 2 for _ in range(chunks)]
-    fillers = {send - 3: raw_filler, send - 2: own_filler, send - 1: sent_filler, send: table_filler}
+    fillers = {send - 3: own_filler, send - 2: raw_filler, send - 1: sent_filler, send: table_filler}
     for s in range(members - 1):
         for j in range(chunks):
             for d in range(2):
@@ -438,7 +450,7 @@
                     arrivals[j][d] = arrived
             if s in fillers:
                 token += tuple(fillers[s](j))
-            if (s, j) == (send - 3, chunks - 1):
+            if (s, j) == (send - 2, chunks - 1):
                 both = jnp.concatenate(raw, axis=1)
                 received = [moved(both[2 * n - 2 : 2 * n], n) for n in range(1, HOPS)]
             if (s, j) == (send - 1, chunks - 1):

time: 136 us -> 129 us (0.949)
  waiting for transfers between devices: 57.5 us -> 45.8 us
  Pallas kernels: 23.9 us -> 29.1 us
    ppermute x28, waiting for transfers between devices: 51.2 us -> 27.9 us  [local(): arrived = lax.ppermute(current[j][d], 'dev', ahead(d, 1))]
    ppermute x12, waiting for transfers between devices: 6.37 us -> 17.9 us  [moved(): parts.append(lax.ppermute(both[d], 'dev', ahead(d, steps)))]
    ppermute x12, starting transfers between devices: 17.9 us -> 13.9 us  [moved(): parts.append(lax.ppermute(both[d], 'dev', ahead(d, steps)))]
    ppermute x28, starting transfers between devices: 28.5 us -> 32.5 us  [local(): arrived = lax.ppermute(current[j][d], 'dev', ahead(d, 1))]
    pallas_call x2, Pallas kernels: 5.11 us -> 7.18 us  [decode_part(): pl.pallas_call(functools.partial(decode_kernel, side, chunk), out_shape=(...]
    pallas_call x4, Pallas kernels: 6.66 us -> 8.62 us  [term_part(): pl.pallas_call(functools.partial(term_kernel, kept, side, members), out_s...]
    pallas_call x2, Pallas kernels: 2.41 us -> 3.81 us  [own_part(): pl.pallas_call(functools.partial(own_kernel, kept, side, members, first),...]
  transfers between devices with their start and end apart: 40 -> 40, of which waited for: 17 -> 12; matrix products, arithmetic and copies ran while one was open for 1% -> 1% of each run, Pallas kernels for 16% -> 21%
where the time goes in v3:
time: 129 us
  starting transfers between devices  46.3 us (36%)
  waiting for transfers between devices  45.8 us (36%)
  Pallas kernels  29.1 us (23%)
  blocking collectives  5.21 us (4%)
    ppermute x28, starting transfers between devices, local(): arrived = lax.ppermute(current[j][d], 'dev', ahead(d, 1))  32.5 us
    ppermute x28, waiting for transfers between devices, local(): arrived = lax.ppermute(current[j][d], 'dev', ahead(d, 1))  27.9 us
    ppermute x12, waiting for transfers between devices, moved(): parts.append(lax.ppermute(both[d], 'dev', ahead(d, steps)))  17.9 us
    ppermute x12, starting transfers between devices, moved(): parts.append(lax.ppermute(both[d], 'dev', ahead(d, steps)))  13.9 us
    pallas_call x4, Pallas kernels, term_part(): pl.pallas_call(functools.partial(term_kernel, kept, side, members), out_s...  8.62 us
    pallas_call x2, Pallas kernels, decode_part(): pl.pallas_call(functools.partial(decode_kernel, side, chunk), out_shape=(...  7.18 us
    pallas_call x6, Pallas kernels, load_part(): pl.pallas_call(functools.partial(load_kernel, members, side, j, s, ways),...  6.09 us
    all_gather x1, blocking collectives, local(): every = lax.all_gather(after(values), 'outer')  5.21 us
  transfers between devices with their start and end apart: 40, of which 12 were waited for; matrix products, arithmetic and copies ran while one was open for 1% of the time, Pallas kernels for 21%

profile of v3, /device:TPU:0, one launch (start us, length us, event | category | flops | bytes accessed | tf_op | source)
XLA Modules:
  0.0 129.0 jit_solution(823311841312708128)
XLA Ops:
  1.7 3.0 %collective-permute-start = (f32[64,1280]{1,0:T(8,128)S(1)}, f32[64,1280]{1,0:T(8,128)S(1)}, u32[]{:S(2)}, u32[]{:S(2)}) collective-permute-start(f32[64,1280]{1,0:T(8,128)S(1)} %get-tuple-element.82), channel_id=1, source_target_pairs={{0,1},{2,0},{4,2},{6,4},{7,6},{5,7},{3,5},{1,3},{8,9},{10,8},{12,1... | collective-permute-start | bytes 983048 | tf_op jit(solution)/shard_map/ppermute | solution.py:441
  5.9 2.0 %collective-permute-start.5 = (f32[64,1280]{1,0:T(8,128)S(1)}, f32[64,1280]{1,0:T(8,128)S(1)}, u32[]{:S(2)}, u32[]{:S(2)}) collective-permute-start(f32[64,1280]{1,0:T(8,128)S(1)} %get-tuple-element.85), channel_id=1, source_target_pairs={{0,2},{2,4},{4,6},{6,7},{7,5},{5,3},{3,1},{1,0},{8,10},{10,12},{12... | collective-permute-start | bytes 983048 | tf_op jit(solution)/shard_map/ppermute | solution.py:441
  10.3 10.7 %collective-permute-done.11 = s32[10,1,128]{2,1,0:T(1,128)S(1)} collective-permute-done((s32[10,1,128]{2,1,0:T(1,128)S(1)}, s32[10,1,128]{2,1,0:T(1,128)S(1)}, u32[]{:S(2)}, u32[]{:S(2)}) %collective-permute-start.11) | collective-permute-done | bytes 5152 | tf_op jit(solution)/shard_map/ppermute | solution.py:394
  31.5 2.1 %collective-permute-done.22 = s32[10,1,128]{2,1,0:T(1,128)S(1)} collective-permute-done((s32[10,1,128]{2,1,0:T(1,128)S(1)}, s32[10,1,128]{2,1,0:T(1,128)S(1)}, u32[]{:S(2)}, u32[]{:S(2)}) %collective-permute-start.22) | collective-permute-done | bytes 5152 | tf_op jit(solution)/shard_map/ppermute | solution.py:394
  40.5 4.8 %collective-permute-done.2 = f32[64,1280]{1,0:T(8,128)S(1)} collective-permute-done((f32[64,1280]{1,0:T(8,128)S(1)}, f32[64,1280]{1,0:T(8,128)S(1)}, u32[]{:S(2)}, u32[]{:S(2)}) %collective-permute-start.2) | collective-permute-done | bytes 327712 | tf_op jit(solution)/shard_map/ppermute | solution.py:441
  47.6 1.9 %shard_map.92 = (f32[128,1280]{1,0:T(8,128)S(1)}, f32[2,5,1,128]{3,2,1,0:T(1,128)S(1)}) custom-call(f32[128,2560]{1,0:T(8,128)S(1)} %bitcast.37, bf16[64,1280]{1,0:T(8,128)(2,1)S(1)} %get-tuple-element.173.refs_0_, bf16[64,1280]{1,0:T(8,128)(2,1)S(1)} %get-tuple-element.172.refs_1_, s32[2,5,1,128]{3,2,1,0:T(1,128)S(1)} %get-tuple-element.101.refs_2_, ...), custom_call_target="tpu_custom_call" | custom-call | flops 419430400 | bytes 1638400 | tf_op jit(solution)/shard_map/pallas_call | solution.py:130
  50.0 2.4 %collective-permute-done.6 = f32[64,1280]{1,0:T(8,128)S(1)} collective-permute-done((f32[64,1280]{1,0:T(8,128)S(1)}, f32[64,1280]{1,0:T(8,128)S(1)}, u32[]{:S(2)}, u32[]{:S(2)}) %collective-permute-start.6) | collective-permute-done | bytes 327712 | tf_op jit(solution)/shard_map/ppermute | solution.py:441
  54.1 1.9 %shard_map.93 = (f32[128,1280]{1,0:T(8,128)S(1)}, f32[2,5,1,128]{3,2,1,0:T(1,128)S(1)}) custom-call(f32[128,2560]{1,0:T(8,128)S(1)} %bitcast.38, bf16[64,1280]{1,0:T(8,128)(2,1)S(1)} %get-tuple-element.171.refs_0_, bf16[64,1280]{1,0:T(8,128)(2,1)S(1)} %get-tuple-element.170.refs_1_, s32[2,5,1,128]{3,2,1,0:T(1,128)S(1)} %get-tuple-element.109.refs_2_, ...), custom_call_target="tpu_custom_call" | custom-call | flops 419430400 | bytes 1638400 | tf_op jit(solution)/shard_map/pallas_call | solution.py:130
  56.1 3.4 %collective-permute-done.8 = f32[64,1280]{1,0:T(8,128)S(1)} collective-permute-done((f32[64,1280]{1,0:T(8,128)S(1)}, f32[64,1280]{1,0:T(8,128)S(1)}, u32[]{:S(2)}, u32[]{:S(2)}) %collective-permute-start.8) | collective-permute-done | bytes 327712 | tf_op jit(solution)/shard_map/ppermute | solution.py:441
  61.6 2.4 %shard_map.94 = f32[4,5,1,128]{3,2,1,0:T(1,128)S(1)} custom-call(bf16[64,1280]{1,0:T(8,128)(2,1)S(1)} %get-tuple-element.169.refs_0_, bf16[64,1280]{1,0:T(8,128)(2,1)S(1)} %get-tuple-element.168.refs_1_, bf16[64,1280]{1,0:T(8,128)(2,1)S(1)} %get-tuple-element.167.refs_2_, bf16[64,1280]{1,0:T(8,128)(2,1)S(1)} %get-tuple-element.166.refs_3_, ...), custom_call_target="tpu_custom_call" | custom-call | flops 1677721600 | bytes 655360 | tf_op jit(solution)/shard_map/pallas_call | solution.py:152
  64.1 2.4 %collective-permute-done.14 = f32[64,1280]{1,0:T(8,128)S(1)} collective-permute-done((f32[64,1280]{1,0:T(8,128)S(1)}, f32[64,1280]{1,0:T(8,128)S(1)}, u32[]{:S(2)}, u32[]{:S(2)}) %collective-permute-start.14) | collective-permute-done | bytes 327712 | tf_op jit(solution)/shard_map/ppermute | solution.py:441
  68.6 2.4 %shard_map.95 = f32[4,5,1,128]{3,2,1,0:T(1,128)S(1)} custom-call(bf16[64,1280]{1,0:T(8,128)(2,1)S(1)} %get-tuple-element.165.refs_0_, bf16[64,1280]{1,0:T(8,128)(2,1)S(1)} %get-tuple-element.164.refs_1_, bf16[64,1280]{1,0:T(8,128)(2,1)S(1)} %get-tuple-element.163.refs_2_, bf16[64,1280]{1,0:T(8,128)(2,1)S(1)} %get-tuple-element.162.refs_3_, ...), custom_call_target="tpu_custom_call" | custom-call | flops 1677721600 | bytes 655360 | tf_op jit(solution)/shard_map/pallas_call | solution.py:152
  74.4 1.9 %shard_map.96 = f32[2,5,1,128]{3,2,1,0:T(1,128)S(1)} custom-call(f32[64,1280]{1,0:T(8,128)S(1)} %convert_add_fusion.11.refs_0_, f32[64,1280]{1,0:T(8,128)S(1)} %convert_add_fusion.10.refs_1_, s32[2,5,1,128]{3,2,1,0:T(1,128)S(1)} %get-tuple-element.128.refs_2_, bf16[3,256,256]{2,1,0:T(8,128)(2,1)S(1)} %copy-done.2, bf16[3,64,64]{2,1,0:T(8,128)(2,1)S(1)} %copy-done.4), custom_call_target="tpu_custom_call" | custom-call | flops 838860800 | bytes 327680 | tf_op jit(solution)/shard_map/pallas_call | solution.py:152
  76.3 2.1 %collective-permute-done.24 = f32[64,1280]{1,0:T(8,128)S(1)} collective-permute-done((f32[64,1280]{1,0:T(8,128)S(1)}, f32[64,1280]{1,0:T(8,128)S(1)}, u32[]{:S(2)}, u32[]{:S(2)}) %collective-permute-start.24) | collective-permute-done | bytes 327712 | tf_op jit(solution)/shard_map/ppermute | solution.py:441
  79.1 2.5 %collective-permute-start.29 = (f32[64,1280]{1,0:T(8,128)S(1)}, f32[64,1280]{1,0:T(8,128)S(1)}, u32[]{:S(2)}, u32[]{:S(2)}) collective-permute-start(f32[64,1280]{1,0:T(8,128)S(1)} %convert_add_fusion.11.refs_0_), channel_id=1, source_target_pairs={{0,2},{2,4},{4,6},{6,7},{7,5},{5,3},{3,1},{1,0},{8,10},{10,12},{12... | collective-permute-start | bytes 983048 | tf_op jit(solution)/shard_map/ppermute | solution.py:441
  81.7 1.9 %shard_map.97 = f32[2,5,1,128]{3,2,1,0:T(1,128)S(1)} custom-call(f32[64,1280]{1,0:T(8,128)S(1)} %convert_add_fusion.9.refs_0_, f32[64,1280]{1,0:T(8,128)S(1)} %convert_add_fusion.8.refs_1_, s32[2,5,1,128]{3,2,1,0:T(1,128)S(1)} %get-tuple-element.133.refs_2_, bf16[3,256,256]{2,1,0:T(8,128)(2,1)S(1)} %copy-done.2, bf16[3,64,64]{2,1,0:T(8,128)(2,1)S(1)} %copy-done.4), custom_call_target="tpu_custom_call" | custom-call | flops 838860800 | bytes 327680 | tf_op jit(solution)/shard_map/pallas_call | solution.py:152
  83.9 3.5 %collective-permute-start.27 = (f32[10,1,128]{2,1,0:T(1,128)S(1)}, f32[10,1,128]{2,1,0:T(1,128)S(1)}, u32[]{:S(2)}, u32[]{:S(2)}) collective-permute-start(f32[10,1,128]{2,1,0:T(1,128)S(1)} %get-tuple-element.183), channel_id=1, source_target_pairs={{0,5},{2,3},{4,1},{6,0},{7,2},{5,4},{3,6},{1,7},{8,13},{10,11},{12... | collective-permute-start | bytes 15368 | tf_op jit(solution)/shard_map/ppermute | solution.py:394
  87.6 2.0 %collective-permute-start.33 = (f32[64,1280]{1,0:T(8,128)S(1)}, f32[64,1280]{1,0:T(8,128)S(1)}, u32[]{:S(2)}, u32[]{:S(2)}) collective-permute-start(f32[64,1280]{1,0:T(8,128)S(1)} %convert_add_fusion.9.refs_0_), channel_id=1, source_target_pairs={{0,2},{2,4},{4,6},{6,7},{7,5},{5,3},{3,1},{1,0},{8,10},{10,12},{12... | collective-permute-start | bytes 983048 | tf_op jit(solution)/shard_map/ppermute | solution.py:441
  93.5 11.7 %collective-permute-done.28 = f32[64,1280]{1,0:T(8,128)S(1)} collective-permute-done((f32[64,1280]{1,0:T(8,128)S(1)}, f32[64,1280]{1,0:T(8,128)S(1)}, u32[]{:S(2)}, u32[]{:S(2)}) %collective-permute-start.28) | collective-permute-done | bytes 327712 | tf_op jit(solution)/shard_map/ppermute | solution.py:441
  106.1 2.1 %collective-permute-start.35 = (f32[64,1280]{1,0:T(8,128)S(1)}, f32[64,1280]{1,0:T(8,128)S(1)}, u32[]{:S(2)}, u32[]{:S(2)}) collective-permute-start(f32[64,1280]{1,0:T(8,128)S(1)} %convert_add_fusion.5), channel_id=1, source_target_pairs={{0,2},{2,4},{4,6},{6,7},{7,5},{5,3},{3,1},{1,0},{8,10},{10,12},{12... | collective-permute-start | bytes 983048 | tf_op jit(solution)/shard_map/ppermute | solution.py:441
  109.2 2.1 %collective-permute-start.38 = (f32[64,1280]{1,0:T(8,128)S(1)}, f32[64,1280]{1,0:T(8,128)S(1)}, u32[]{:S(2)}, u32[]{:S(2)}) collective-permute-start(f32[64,1280]{1,0:T(8,128)S(1)} %convert_add_fusion.3), channel_id=1, source_target_pairs={{0,2},{2,4},{4,6},{6,7},{7,5},{5,3},{3,1},{1,0},{8,10},{10,12},{12... | collective-permute-start | bytes 983048 | tf_op jit(solution)/shard_map/ppermute | solution.py:441
  112.4 5.2 %all-gather = f32[8,10,1,128]{3,2,1,0:T(1,128)S(1)} all-gather(f32[2,10,1,128]{3,2,1,0:T(1,128)S(1)} %maximum_add_fusion), channel_id=2, replica_groups=mesh['outer'=4,'dev'=8] {'outer'}, dimensions={0}, use_global_device_ids=true | all-gather | bytes 51200 | tf_op jit(solution)/shard_map/all_gather | solution.py:460
  119.8 3.5 %shard_map.100 = (f32[128,2560]{1,0:T(8,128)}, f32[128,1280]{1,0:T(8,128)S(1)}) custom-call(s32[1]{0:T(128)} %bitcast.pod_ref, f32[4,2,10,1,128]{4,3,2,1,0:T(1,128)S(1)} %bitcast.39, f32[2,5,64,512]{3,2,1,0:T(8,128)S(1)} %get-tuple-element.139.rows_ref, bf16[2,5,512,256]{3,2,1,0:T(8,128)(2,1)S(1)} %get-tuple-element.140.cols_ref, ...), custom_call_target="tpu_custom_call" | custom-call | flops 838860800 | bytes 1966080 | tf_op jit(solution)/shard_map/pallas_call | solution.py:229
  123.4 3.7 %shard_map.101 = (f32[128,2560]{1,0:T(8,128)}, f32[128,1280]{1,0:T(8,128)S(1)}) custom-call(s32[1]{0:T(128)} %bitcast.pod_ref, f32[4,2,10,1,128]{4,3,2,1,0:T(1,128)S(1)} %bitcast.40, f32[2,5,64,512]{3,2,1,0:T(8,128)S(1)} %get-tuple-element.146.rows_ref, bf16[2,5,512,256]{3,2,1,0:T(8,128)(2,1)S(1)} %get-tuple-element.147.cols_ref, ...), custom_call_target="tpu_custom_call", output_to_operand_aliasing={{0}: (7, {})} | custom-call | flops 838860800 | bytes 1966080 | tf_op jit(solution)/shard_map/pallas_call | solution.py:229
  (129 shorter events, 46.1 us)
Async XLA Ops:
  1.7 31.9 %collective-permute-start = (f32[64,1280]{1,0:T(8,128)S(1)}, f32[64,1280]{1,0:T(8,128)S(1)}, u32[]{:S(2)}, u32[]{:S(2)}) collective-permute-start(f32[64,1280]{1,0:T(8,128)S(1)} %get-tuple-element.82), channel_id=1, source_target_pairs={{0,1},{2,0},{4,2},{6,4},{7,6},{5,7},{3,5},{1,3},{8,9},{10,8},{12,1... | collective-permute-start | bytes 983048 | tf_op jit(solution)/shard_map/ppermute | solution.py:441
  4.8 21.5 %collective-permute-start.1 = (f32[64,1280]{1,0:T(8,128)S(1)}, f32[64,1280]{1,0:T(8,128)S(1)}, u32[]{:S(2)}, u32[]{:S(2)}) collective-permute-start(f32[64,1280]{1,0:T(8,128)S(1)} %get-tuple-element.83), channel_id=1, source_target_pairs={{0,2},{2,4},{4,6},{6,7},{7,5},{5,3},{3,1},{1,0},{8,10},{10,12},{12... | collective-permute-start | bytes 983048 | tf_op jit(solution)/shard_map/ppermute | solution.py:441
  5.9 30.4 %collective-permute-start.5 = (f32[64,1280]{1,0:T(8,128)S(1)}, f32[64,1280]{1,0:T(8,128)S(1)}, u32[]{:S(2)}, u32[]{:S(2)}) collective-permute-start(f32[64,1280]{1,0:T(8,128)S(1)} %get-tuple-element.85), channel_id=1, source_target_pairs={{0,2},{2,4},{4,6},{6,7},{7,5},{5,3},{3,1},{1,0},{8,10},{10,12},{12... | collective-permute-start | bytes 983048 | tf_op jit(solution)/shard_map/ppermute | solution.py:441
  8.2 12.8 %collective-permute-start.11 = (s32[10,1,128]{2,1,0:T(1,128)S(1)}, s32[10,1,128]{2,1,0:T(1,128)S(1)}, u32[]{:S(2)}, u32[]{:S(2)}) collective-permute-start(s32[10,1,128]{2,1,0:T(1,128)S(1)} %get-tuple-element.176), channel_id=1, source_target_pairs={{0,2},{2,4},{4,6},{6,7},{7,5},{5,3},{3,1},{1,0},{8,10},{10,12},{12... | collective-permute-start | bytes 15368 | tf_op jit(solution)/shard_map/ppermute | solution.py:394
  9.9 11.6 %collective-permute-start.10 = (s32[10,1,128]{2,1,0:T(1,128)S(1)}, s32[10,1,128]{2,1,0:T(1,128)S(1)}, u32[]{:S(2)}, u32[]{:S(2)}) collective-permute-start(s32[10,1,128]{2,1,0:T(1,128)S(1)} %get-tuple-element.177), channel_id=1, source_target_pairs={{0,1},{2,0},{4,2},{6,4},{7,6},{5,7},{3,5},{1,3},{8,9},{10,8},{12,1... | collective-permute-start | bytes 15368 | tf_op jit(solution)/shard_map/ppermute | solution.py:394
  24.7 13.2 %collective-permute-start.4 = (f32[64,1280]{1,0:T(8,128)S(1)}, f32[64,1280]{1,0:T(8,128)S(1)}, u32[]{:S(2)}, u32[]{:S(2)}) collective-permute-start(f32[64,1280]{1,0:T(8,128)S(1)} %get-tuple-element.86), channel_id=1, source_target_pairs={{0,1},{2,0},{4,2},{6,4},{7,6},{5,7},{3,5},{1,3},{8,9},{10,8},{12,1... | collective-permute-start | bytes 983048 | tf_op jit(solution)/shard_map/ppermute | solution.py:441
  27.7 12.8 %collective-permute-start.3 = (f32[64,1280]{1,0:T(8,128)S(1)}, f32[64,1280]{1,0:T(8,128)S(1)}, u32[]{:S(2)}, u32[]{:S(2)}) collective-permute-start(f32[64,1280]{1,0:T(8,128)S(1)} %shard_map.88), channel_id=1, source_target_pairs={{0,2},{2,4},{4,6},{6,7},{7,5},{5,3},{3,1},{1,0},{8,10},{10,12},{12... | collective-permute-start | bytes 983048 | tf_op jit(solution)/shard_map/ppermute | solution.py:441
  37.4 12.1 %collective-permute-start.7 = (f32[64,1280]{1,0:T(8,128)S(1)}, f32[64,1280]{1,0:T(8,128)S(1)}, u32[]{:S(2)}, u32[]{:S(2)}) collective-permute-start(f32[64,1280]{1,0:T(8,128)S(1)} %shard_map.90), channel_id=1, source_target_pairs={{0,2},{2,4},{4,6},{6,7},{7,5},{5,3},{3,1},{1,0},{8,10},{10,12},{12... | collective-permute-start | bytes 983048 | tf_op jit(solution)/shard_map/ppermute | solution.py:441
  38.8 13.6 %collective-permute-start.6 = (f32[64,1280]{1,0:T(8,128)S(1)}, f32[64,1280]{1,0:T(8,128)S(1)}, u32[]{:S(2)}, u32[]{:S(2)}) collective-permute-start(f32[64,1280]{1,0:T(8,128)S(1)} %shard_map.91), channel_id=1, source_target_pairs={{0,1},{2,0},{4,2},{6,4},{7,6},{5,7},{3,5},{1,3},{8,9},{10,8},{12,1... | collective-permute-start | bytes 983048 | tf_op jit(solution)/shard_map/ppermute | solution.py:441
  45.4 14.0 %collective-permute-start.8 = (f32[64,1280]{1,0:T(8,128)S(1)}, f32[64,1280]{1,0:T(8,128)S(1)}, u32[]{:S(2)}, u32[]{:S(2)}) collective-permute-start(f32[64,1280]{1,0:T(8,128)S(1)} %convert_add_fusion.18), channel_id=1, source_target_pairs={{0,1},{2,0},{4,2},{6,4},{7,6},{5,7},{3,5},{1,3},{8,9},{10,8},{12,1... | collective-permute-start | bytes 983048 | tf_op jit(solution)/shard_map/ppermute | solution.py:441
  49.5 14.5 %collective-permute-start.15 = (f32[64,1280]{1,0:T(8,128)S(1)}, f32[64,1280]{1,0:T(8,128)S(1)}, u32[]{:S(2)}, u32[]{:S(2)}) collective-permute-start(f32[64,1280]{1,0:T(8,128)S(1)} %convert_add_fusion.17), channel_id=1, source_target_pairs={{0,2},{2,4},{4,6},{6,7},{7,5},{5,3},{3,1},{1,0},{8,10},{10,12},{12... | collective-permute-start | bytes 983048 | tf_op jit(solution)/shard_map/ppermute | solution.py:441
  52.4 14.0 %collective-permute-start.14 = (f32[64,1280]{1,0:T(8,128)S(1)}, f32[64,1280]{1,0:T(8,128)S(1)}, u32[]{:S(2)}, u32[]{:S(2)}) collective-permute-start(f32[64,1280]{1,0:T(8,128)S(1)} %convert_add_fusion.16), channel_id=1, source_target_pairs={{0,1},{2,0},{4,2},{6,4},{7,6},{5,7},{3,5},{1,3},{8,9},{10,8},{12,1... | collective-permute-start | bytes 983048 | tf_op jit(solution)/shard_map/ppermute | solution.py:441
  59.5 14.2 %collective-permute-start.21 = (f32[64,1280]{1,0:T(8,128)S(1)}, f32[64,1280]{1,0:T(8,128)S(1)}, u32[]{:S(2)}, u32[]{:S(2)}) collective-permute-start(f32[64,1280]{1,0:T(8,128)S(1)} %convert_add_fusion.14), channel_id=1, source_target_pairs={{0,1},{2,0},{4,2},{6,4},{7,6},{5,7},{3,5},{1,3},{8,9},{10,8},{12,1... | collective-permute-start | bytes 983048 | tf_op jit(solution)/shard_map/ppermute | solution.py:441
  66.5 12.6 %collective-permute-start.25 = (f32[64,1280]{1,0:T(8,128)S(1)}, f32[64,1280]{1,0:T(8,128)S(1)}, u32[]{:S(2)}, u32[]{:S(2)}) collective-permute-start(f32[64,1280]{1,0:T(8,128)S(1)} %convert_add_fusion.12), channel_id=1, source_target_pairs={{0,1},{2,0},{4,2},{6,4},{7,6},{5,7},{3,5},{1,3},{8,9},{10,8},{12,1... | collective-permute-start | bytes 983048 | tf_op jit(solution)/shard_map/ppermute | solution.py:441
  71.1 12.5 %collective-permute-start.18 = (f32[10,1,128]{2,1,0:T(1,128)S(1)}, f32[10,1,128]{2,1,0:T(1,128)S(1)}, u32[]{:S(2)}, u32[]{:S(2)}) collective-permute-start(f32[10,1,128]{2,1,0:T(1,128)S(1)} %get-tuple-element.178), channel_id=1, source_target_pairs={{0,4},{2,6},{4,7},{6,5},{7,3},{5,1},{3,0},{1,2},{8,12},{10,14},{12... | collective-permute-start | bytes 15368 | tf_op jit(solution)/shard_map/ppermute | solution.py:394
  72.1 11.9 %collective-permute-start.16 = (f32[10,1,128]{2,1,0:T(1,128)S(1)}, f32[10,1,128]{2,1,0:T(1,128)S(1)}, u32[]{:S(2)}, u32[]{:S(2)}) collective-permute-start(f32[10,1,128]{2,1,0:T(1,128)S(1)} %get-tuple-element.179), channel_id=1, source_target_pairs={{0,2},{2,4},{4,6},{6,7},{7,5},{5,3},{3,1},{1,0},{8,10},{10,12},{12... | collective-permute-start | bytes 15368 | tf_op jit(solution)/shard_map/ppermute | solution.py:394
  73.7 13.8 %collective-permute-start.17 = (f32[10,1,128]{2,1,0:T(1,128)S(1)}, f32[10,1,128]{2,1,0:T(1,128)S(1)}, u32[]{:S(2)}, u32[]{:S(2)}) collective-permute-start(f32[10,1,128]{2,1,0:T(1,128)S(1)} %get-tuple-element.180), channel_id=1, source_target_pairs={{0,1},{2,0},{4,2},{6,4},{7,6},{5,7},{3,5},{1,3},{8,9},{10,8},{12,1... | collective-permute-start | bytes 15368 | tf_op jit(solution)/shard_map/ppermute | solution.py:394
  79.1 12.7 %collective-permute-start.29 = (f32[64,1280]{1,0:T(8,128)S(1)}, f32[64,1280]{1,0:T(8,128)S(1)}, u32[]{:S(2)}, u32[]{:S(2)}) collective-permute-start(f32[64,1280]{1,0:T(8,128)S(1)} %convert_add_fusion.11.refs_0_), channel_id=1, source_target_pairs={{0,2},{2,4},{4,6},{6,7},{7,5},{5,3},{3,1},{1,0},{8,10},{10,12},{12... | collective-permute-start | bytes 983048 | tf_op jit(solution)/shard_map/ppermute | solution.py:441
  87.5 20.7 %collective-permute-start.32 = (f32[64,1280]{1,0:T(8,128)S(1)}, f32[64,1280]{1,0:T(8,128)S(1)}, u32[]{:S(2)}, u32[]{:S(2)}) collective-permute-start(f32[64,1280]{1,0:T(8,128)S(1)} %convert_add_fusion.8.refs_1_), channel_id=1, source_target_pairs={{0,1},{2,0},{4,2},{6,4},{7,6},{5,7},{3,5},{1,3},{8,9},{10,8},{12,1... | collective-permute-start | bytes 983048 | tf_op jit(solution)/shard_map/ppermute | solution.py:441
  87.6 18.5 %collective-permute-start.33 = (f32[64,1280]{1,0:T(8,128)S(1)}, f32[64,1280]{1,0:T(8,128)S(1)}, u32[]{:S(2)}, u32[]{:S(2)}) collective-permute-start(f32[64,1280]{1,0:T(8,128)S(1)} %convert_add_fusion.9.refs_0_), channel_id=1, source_target_pairs={{0,2},{2,4},{4,6},{6,7},{7,5},{5,3},{3,1},{1,0},{8,10},{10,12},{12... | collective-permute-start | bytes 983048 | tf_op jit(solution)/shard_map/ppermute | solution.py:441
  91.3 13.9 %collective-permute-start.28 = (f32[64,1280]{1,0:T(8,128)S(1)}, f32[64,1280]{1,0:T(8,128)S(1)}, u32[]{:S(2)}, u32[]{:S(2)}) collective-permute-start(f32[64,1280]{1,0:T(8,128)S(1)} %convert_add_fusion.10.refs_1_), channel_id=1, source_target_pairs={{0,1},{2,0},{4,2},{6,4},{7,6},{5,7},{3,5},{1,3},{8,9},{10,8},{12,1... | collective-permute-start | bytes 983048 | tf_op jit(solution)/shard_map/ppermute | solution.py:441
  91.8 17.4 %collective-permute-start.31 = (f32[64,1280]{1,0:T(8,128)S(1)}, f32[64,1280]{1,0:T(8,128)S(1)}, u32[]{:S(2)}, u32[]{:S(2)}) collective-permute-start(f32[64,1280]{1,0:T(8,128)S(1)} %convert_add_fusion.7), channel_id=1, source_target_pairs={{0,2},{2,4},{4,6},{6,7},{7,5},{5,3},{3,1},{1,0},{8,10},{10,12},{12... | collective-permute-start | bytes 983048 | tf_op jit(solution)/shard_map/ppermute | solution.py:441
  109.2 17.9 %collective-permute-start.38 = (f32[64,1280]{1,0:T(8,128)S(1)}, f32[64,1280]{1,0:T(8,128)S(1)}, u32[]{:S(2)}, u32[]{:S(2)}) collective-permute-start(f32[64,1280]{1,0:T(8,128)S(1)} %convert_add_fusion.3), channel_id=1, source_target_pairs={{0,2},{2,4},{4,6},{6,7},{7,5},{5,3},{3,1},{1,0},{8,10},{10,12},{12... | collective-permute-start | bytes 983048 | tf_op jit(solution)/shard_map/ppermute | solution.py:441
  112.4 14.7 %collective-permute-start.39 = (f32[64,1280]{1,0:T(8,128)S(1)}, f32[64,1280]{1,0:T(8,128)S(1)}, u32[]{:S(2)}, u32[]{:S(2)}) collective-permute-start(f32[64,1280]{1,0:T(8,128)S(1)} %convert_add_fusion.2), channel_id=1, source_target_pairs={{0,1},{2,0},{4,2},{6,4},{7,6},{5,7},{3,5},{1,3},{8,9},{10,8},{12,1... | collective-permute-start | bytes 983048 | tf_op jit(solution)/shard_map/ppermute | solution.py:441
  (24 other events, 257.5 us)

commit v4 on v3

--- a/solution.py
+++ b/solution.py
@@ -282,6 +282,48 @@
     return jnp.where(q < members // 2, 2 * q, 2 * members - 1 - 2 * q)
 
 
+def stage_kernel(members, side, j, s, ways, grad_ref, *refs):
+    out_refs, sem_ref = refs[:-1], refs[-1]
+    width = out_refs[0].shape[1]
+    position = ring_position(members)
+    chunks = grad_ref.shape[1] // (members * width)
+    copies = []
+    for i, d in enumerate(ways):
+        start = pl.multiple_of((ring_owner(position, d, s, members) * chunks + j) * width, LANES)
+        source = grad_ref.at[pl.ds(d * side, side), pl.ds(start, width)]
+        copies.append(pltpu.make_async_copy(source, out_refs[i], sem_ref.at[i]))
+        copies[-1].start()
+    for copy in copies:
+        copy.wait()
+
+
+def stage_part(grad, ways, j, s, members, side, width):
+    return pl.pallas_call(
+        functools.partial(stage_kernel, members, side, j, s, ways),
+        out_shape=[pltpu.VMEM((side, width), grad.dtype) for _ in ways],
+        in_specs=[pl.BlockSpec(memory_space=pl.ANY)],
+        out_specs=[ON_CHIP] * len(ways),
+        scratch_shapes=[pltpu.SemaphoreType.DMA((len(ways),))],
+        compiler_params=PARAMS,
+        cost_estimate=cost(0, side * width * 4 * len(ways)),
+    )(grad)
+
+
+def join_kernel(arrived_ref, term_ref, out_ref):
+    out_ref[...] = arrived_ref[...] + term_ref[...].astype(f32)
+
+
+def join_part(arrived, term):
+    return pl.pallas_call(
+        join_kernel,
+        out_shape=pltpu.VMEM(arrived.shape, f32),
+        in_specs=[ON_CHIP] * 2,
+        out_specs=ON_CHIP,
+        compiler_params=PARAMS,
+        cost_estimate=cost(arrived.size, arrived.size * 10),
+    )(in_vmem(arrived), in_vmem(term))
+
+
 def load_kernel(members, side, j, s, ways, grad_ref, *refs):
     out_refs, (buffer_ref, sem_ref) = refs[-2 - len(ways) : -2], refs[-2:]
     arrived_refs = refs[: -2 - len(ways)]
@@ -388,6 +430,14 @@
     def after(array):
         return tie(array, *token)[0]
 
+    second = [None] * chunks
+
+    def stage(j):
+        second[j] = stage_part(after(in_hbm(grad)), (0, 1), j, 1, members, side, piece_cols)
+        return tuple(second[j])
+
+    token = stage(0)
+
     def moved(both, steps):
         parts = []
         for d in range(2):
@@ -442,12 +492,14 @@
                 if s < last:
                     arrived, source, *_ = tie(arrived, grad, *token)
                     if s == 0:
-                        (current[j][d],) = load(in_hbm(source), (arrived,), (d,), j, s + 1)
+                        current[j][d] = join_part(arrived, second[j][d])
                     else:
                         current[j][d] = arrived + piece(source, d, s + 1, j).astype(f32)
                     token = (current[j][d],)
                 else:
                     arrivals[j][d] = arrived
+            if s == 0 and j + 1 < chunks:
+                token += stage(j + 1)
             if s in fillers:
                 token += tuple(fillers[s](j))
             if (s, j) == (send - 2, chunks - 1):
@@ -461,7 +513,9 @@
                 token += (every,)
     update, rests = None, []
     for j in range(chunks):
-        update, rest = decode_part(pod[None], after(every), tables[j], own[j][0], wide, same, side, j, chunks, update)
+        update, rest = decode_part(
+            pod[None], after(every), tables[j], own[j][0], wide, same, side, j, chunks, update
+        )
         rests.append(rest)
     out = None
     for j in range(chunks):

time: 129 us -> 128 us (level)
  Pallas kernels: 29.1 us -> 27 us
  other arithmetic: 0.84 us -> 2.63 us
  waiting for transfers between devices: 45.8 us -> 44.4 us
    pallas_call x6 -> x2, Pallas kernels: 6.09 us -> 2.08 us  [load_part(): pl.pallas_call(functools.partial(load_kernel, members, side, j, s, ways),...]
    pallas_call x0 -> x6, Pallas kernels: none -> 2.14 us  [the longest x2 2.02 us: stage_part(): pl.pallas_call(functools.partial(stage_kernel, members, side, j, s, ways)...]
    ppermute x28, waiting for transfers between devices: 27.9 us -> 25.8 us  [local(): arrived = lax.ppermute(current[j][d], 'dev', ahead(d, 1))]
    add x20, other arithmetic: 0.76 us -> 2.55 us  [local(): current[j][d] = arrived + piece(source, d, s + 1, j).astype(f32)]
  transfers between devices with their start and end apart: 40 -> 40, of which waited for: 12 -> 16; matrix products, arithmetic and copies ran while one was open for 1% -> 3% of each run, Pallas kernels for 21% -> 20%
where the time goes in v4:
time: 128 us
  starting transfers between devices  45.9 us (36%)
  waiting for transfers between devices  44.4 us (35%)
  Pallas kernels  27 us (21%)
  blocking collectives  5.21 us (4%)
  other arithmetic  2.63 us (2%)
  local copies, waits for them, and re-layouts  1.46 us (1%)
  between operations  1.3 us (1%)
    ppermute x28, starting transfers between devices, local(): arrived = lax.ppermute(current[j][d], 'dev', ahead(d, 1))  32.4 us
    ppermute x28, waiting for transfers between devices, local(): arrived = lax.ppermute(current[j][d], 'dev', ahead(d, 1))  25.8 us
    ppermute x12, waiting for transfers between devices, moved(): parts.append(lax.ppermute(both[d], 'dev', ahead(d, steps)))  18.5 us
    ppermute x12, starting transfers between devices, moved(): parts.append(lax.ppermute(both[d], 'dev', ahead(d, steps)))  13.4 us
    pallas_call x4, Pallas kernels, term_part(): pl.pallas_call(functools.partial(term_kernel, kept, side, members), out_s...  8.61 us
    pallas_call x2, Pallas kernels, decode_part(): pl.pallas_call(functools.partial(decode_kernel, side, chunk), out_shape=(...  6.94 us
    all_gather x1, blocking collectives, local(): every = lax.all_gather(after(values), 'outer')  5.21 us
    pallas_call x2, Pallas kernels, own_part(): pl.pallas_call(functools.partial(own_kernel, kept, side, members, first),...  3.79 us
  transfers between devices with their start and end apart: 40, of which 16 were waited for; matrix products, arithmetic and copies ran while one was open for 3% of the time, Pallas kernels for 20%

profile of v4, /device:TPU:0, one launch (start us, length us, event | category | flops | bytes accessed | tf_op | source)
XLA Modules:
  0.0 127.8 jit_solution(163717660621901914)
XLA Ops:
  1.7 3.0 %collective-permute-start = (f32[64,1280]{1,0:T(8,128)S(1)}, f32[64,1280]{1,0:T(8,128)S(1)}, u32[]{:S(2)}, u32[]{:S(2)}) collective-permute-start(f32[64,1280]{1,0:T(8,128)S(1)} %get-tuple-element.84), channel_id=1, source_target_pairs={{0,1},{2,0},{4,2},{6,4},{7,6},{5,7},{3,5},{1,3},{8,9},{10,8},{12,1... | collective-permute-start | bytes 983048 | tf_op jit(solution)/shard_map/ppermute | solution.py:491
  5.9 2.0 %collective-permute-start.5 = (f32[64,1280]{1,0:T(8,128)S(1)}, f32[64,1280]{1,0:T(8,128)S(1)}, u32[]{:S(2)}, u32[]{:S(2)}) collective-permute-start(f32[64,1280]{1,0:T(8,128)S(1)} %get-tuple-element.87), channel_id=1, source_target_pairs={{0,2},{2,4},{4,6},{6,7},{7,5},{5,3},{3,1},{1,0},{8,10},{10,12},{12... | collective-permute-start | bytes 983048 | tf_op jit(solution)/shard_map/ppermute | solution.py:491
  11.3 9.7 %collective-permute-done.11 = s32[10,1,128]{2,1,0:T(1,128)S(1)} collective-permute-done((s32[10,1,128]{2,1,0:T(1,128)S(1)}, s32[10,1,128]{2,1,0:T(1,128)S(1)}, u32[]{:S(2)}, u32[]{:S(2)}) %collective-permute-start.11) | collective-permute-done | bytes 5152 | tf_op jit(solution)/shard_map/ppermute | solution.py:444
  27.2 2.6 %collective-permute-done.23 = s32[10,1,128]{2,1,0:T(1,128)S(1)} collective-permute-done((s32[10,1,128]{2,1,0:T(1,128)S(1)}, s32[10,1,128]{2,1,0:T(1,128)S(1)}, u32[]{:S(2)}, u32[]{:S(2)}) %collective-permute-start.23) | collective-permute-done | bytes 5152 | tf_op jit(solution)/shard_map/ppermute | solution.py:444
  31.5 2.1 %collective-permute-done.22 = s32[10,1,128]{2,1,0:T(1,128)S(1)} collective-permute-done((s32[10,1,128]{2,1,0:T(1,128)S(1)}, s32[10,1,128]{2,1,0:T(1,128)S(1)}, u32[]{:S(2)}, u32[]{:S(2)}) %collective-permute-start.22) | collective-permute-done | bytes 5152 | tf_op jit(solution)/shard_map/ppermute | solution.py:444
  39.4 4.8 %collective-permute-done.2 = f32[64,1280]{1,0:T(8,128)S(1)} collective-permute-done((f32[64,1280]{1,0:T(8,128)S(1)}, f32[64,1280]{1,0:T(8,128)S(1)}, u32[]{:S(2)}, u32[]{:S(2)}) %collective-permute-start.2) | collective-permute-done | bytes 327712 | tf_op jit(solution)/shard_map/ppermute | solution.py:491
  48.3 1.9 %shard_map.94 = (f32[128,1280]{1,0:T(8,128)S(1)}, f32[2,5,1,128]{3,2,1,0:T(1,128)S(1)}) custom-call(f32[128,2560]{1,0:T(8,128)S(1)} %bitcast.37, bf16[64,1280]{1,0:T(8,128)(2,1)S(1)} %get-tuple-element.177.refs_0_, bf16[64,1280]{1,0:T(8,128)(2,1)S(1)} %get-tuple-element.176.refs_1_, s32[2,5,1,128]{3,2,1,0:T(1,128)S(1)} %get-tuple-element.105.refs_2_, ...), custom_call_target="tpu_custom_call" | custom-call | flops 419430400 | bytes 1638400 | tf_op jit(solution)/shard_map/pallas_call | solution.py:130
  53.0 1.9 %shard_map.95 = (f32[128,1280]{1,0:T(8,128)S(1)}, f32[2,5,1,128]{3,2,1,0:T(1,128)S(1)}) custom-call(f32[128,2560]{1,0:T(8,128)S(1)} %bitcast.38, bf16[64,1280]{1,0:T(8,128)(2,1)S(1)} %get-tuple-element.175.refs_0_, bf16[64,1280]{1,0:T(8,128)(2,1)S(1)} %get-tuple-element.174.refs_1_, s32[2,5,1,128]{3,2,1,0:T(1,128)S(1)} %get-tuple-element.113.refs_2_, ...), custom_call_target="tpu_custom_call" | custom-call | flops 419430400 | bytes 1638400 | tf_op jit(solution)/shard_map/pallas_call | solution.py:130
  56.1 2.2 %collective-permute-done.8 = f32[64,1280]{1,0:T(8,128)S(1)} collective-permute-done((f32[64,1280]{1,0:T(8,128)S(1)}, f32[64,1280]{1,0:T(8,128)S(1)}, u32[]{:S(2)}, u32[]{:S(2)}) %collective-permute-start.8) | collective-permute-done | bytes 327712 | tf_op jit(solution)/shard_map/ppermute | solution.py:491
  60.5 2.4 %shard_map.96 = f32[4,5,1,128]{3,2,1,0:T(1,128)S(1)} custom-call(bf16[64,1280]{1,0:T(8,128)(2,1)S(1)} %get-tuple-element.173.refs_0_, bf16[64,1280]{1,0:T(8,128)(2,1)S(1)} %get-tuple-element.172.refs_1_, bf16[64,1280]{1,0:T(8,128)(2,1)S(1)} %get-tuple-element.171.refs_2_, bf16[64,1280]{1,0:T(8,128)(2,1)S(1)} %get-tuple-element.170.refs_3_, ...), custom_call_target="tpu_custom_call" | custom-call | flops 1677721600 | bytes 655360 | tf_op jit(solution)/shard_map/pallas_call | solution.py:152
  63.2 2.2 %collective-permute-done.14 = f32[64,1280]{1,0:T(8,128)S(1)} collective-permute-done((f32[64,1280]{1,0:T(8,128)S(1)}, f32[64,1280]{1,0:T(8,128)S(1)}, u32[]{:S(2)}, u32[]{:S(2)}) %collective-permute-start.14) | collective-permute-done | bytes 327712 | tf_op jit(solution)/shard_map/ppermute | solution.py:491
  67.5 2.4 %shard_map.97 = f32[4,5,1,128]{3,2,1,0:T(1,128)S(1)} custom-call(bf16[64,1280]{1,0:T(8,128)(2,1)S(1)} %get-tuple-element.169.refs_0_, bf16[64,1280]{1,0:T(8,128)(2,1)S(1)} %get-tuple-element.168.refs_1_, bf16[64,1280]{1,0:T(8,128)(2,1)S(1)} %get-tuple-element.167.refs_2_, bf16[64,1280]{1,0:T(8,128)(2,1)S(1)} %get-tuple-element.166.refs_3_, ...), custom_call_target="tpu_custom_call" | custom-call | flops 1677721600 | bytes 655360 | tf_op jit(solution)/shard_map/pallas_call | solution.py:152
  72.8 1.9 %shard_map.98 = f32[2,5,1,128]{3,2,1,0:T(1,128)S(1)} custom-call(f32[64,1280]{1,0:T(8,128)S(1)} %convert_add_fusion.11.refs_0_, f32[64,1280]{1,0:T(8,128)S(1)} %convert_add_fusion.10.refs_1_, s32[2,5,1,128]{3,2,1,0:T(1,128)S(1)} %get-tuple-element.132.refs_2_, bf16[3,256,256]{2,1,0:T(8,128)(2,1)S(1)} %copy-done.2, bf16[3,64,64]{2,1,0:T(8,128)(2,1)S(1)} %copy-done.4), custom_call_target="tpu_custom_call" | custom-call | flops 838860800 | bytes 327680 | tf_op jit(solution)/shard_map/pallas_call | solution.py:152
  77.3 2.5 %collective-permute-start.29 = (f32[64,1280]{1,0:T(8,128)S(1)}, f32[64,1280]{1,0:T(8,128)S(1)}, u32[]{:S(2)}, u32[]{:S(2)}) collective-permute-start(f32[64,1280]{1,0:T(8,128)S(1)} %convert_add_fusion.11.refs_0_), channel_id=1, source_target_pairs={{0,2},{2,4},{4,6},{6,7},{7,5},{5,3},{3,1},{1,0},{8,10},{10,12},{12... | collective-permute-start | bytes 983048 | tf_op jit(solution)/shard_map/ppermute | solution.py:491
  79.8 1.9 %shard_map.99 = f32[2,5,1,128]{3,2,1,0:T(1,128)S(1)} custom-call(f32[64,1280]{1,0:T(8,128)S(1)} %convert_add_fusion.9.refs_0_, f32[64,1280]{1,0:T(8,128)S(1)} %convert_add_fusion.8.refs_1_, s32[2,5,1,128]{3,2,1,0:T(1,128)S(1)} %get-tuple-element.137.refs_2_, bf16[3,256,256]{2,1,0:T(8,128)(2,1)S(1)} %copy-done.2, bf16[3,64,64]{2,1,0:T(8,128)(2,1)S(1)} %copy-done.4), custom_call_target="tpu_custom_call" | custom-call | flops 838860800 | bytes 327680 | tf_op jit(solution)/shard_map/pallas_call | solution.py:152
  82.5 3.2 %collective-permute-start.27 = (f32[10,1,128]{2,1,0:T(1,128)S(1)}, f32[10,1,128]{2,1,0:T(1,128)S(1)}, u32[]{:S(2)}, u32[]{:S(2)}) collective-permute-start(f32[10,1,128]{2,1,0:T(1,128)S(1)} %get-tuple-element.187), channel_id=1, source_target_pairs={{0,5},{2,3},{4,1},{6,0},{7,2},{5,4},{3,6},{1,7},{8,13},{10,11},{12... | collective-permute-start | bytes 15368 | tf_op jit(solution)/shard_map/ppermute | solution.py:444
  85.7 2.0 %collective-permute-start.33 = (f32[64,1280]{1,0:T(8,128)S(1)}, f32[64,1280]{1,0:T(8,128)S(1)}, u32[]{:S(2)}, u32[]{:S(2)}) collective-permute-start(f32[64,1280]{1,0:T(8,128)S(1)} %convert_add_fusion.9.refs_0_), channel_id=1, source_target_pairs={{0,2},{2,4},{4,6},{6,7},{7,5},{5,3},{3,1},{1,0},{8,10},{10,12},{12... | collective-permute-start | bytes 983048 | tf_op jit(solution)/shard_map/ppermute | solution.py:491
  87.7 2.5 %collective-permute-done.26 = f32[10,1,128]{2,1,0:T(1,128)S(1)} collective-permute-done((f32[10,1,128]{2,1,0:T(1,128)S(1)}, f32[10,1,128]{2,1,0:T(1,128)S(1)}, u32[]{:S(2)}, u32[]{:S(2)}) %collective-permute-start.26) | collective-permute-done | bytes 5152 | tf_op jit(solution)/shard_map/ppermute | solution.py:444
  92.4 10.9 %collective-permute-done.28 = f32[64,1280]{1,0:T(8,128)S(1)} collective-permute-done((f32[64,1280]{1,0:T(8,128)S(1)}, f32[64,1280]{1,0:T(8,128)S(1)}, u32[]{:S(2)}, u32[]{:S(2)}) %collective-permute-start.28) | collective-permute-done | bytes 327712 | tf_op jit(solution)/shard_map/ppermute | solution.py:491
  104.3 2.1 %collective-permute-start.35 = (f32[64,1280]{1,0:T(8,128)S(1)}, f32[64,1280]{1,0:T(8,128)S(1)}, u32[]{:S(2)}, u32[]{:S(2)}) collective-permute-start(f32[64,1280]{1,0:T(8,128)S(1)} %convert_add_fusion.5), channel_id=1, source_target_pairs={{0,2},{2,4},{4,6},{6,7},{7,5},{5,3},{3,1},{1,0},{8,10},{10,12},{12... | collective-permute-start | bytes 983048 | tf_op jit(solution)/shard_map/ppermute | solution.py:491
  107.3 2.1 %collective-permute-start.38 = (f32[64,1280]{1,0:T(8,128)S(1)}, f32[64,1280]{1,0:T(8,128)S(1)}, u32[]{:S(2)}, u32[]{:S(2)}) collective-permute-start(f32[64,1280]{1,0:T(8,128)S(1)} %convert_add_fusion.3), channel_id=1, source_target_pairs={{0,2},{2,4},{4,6},{6,7},{7,5},{5,3},{3,1},{1,0},{8,10},{10,12},{12... | collective-permute-start | bytes 983048 | tf_op jit(solution)/shard_map/ppermute | solution.py:491
  110.6 5.2 %all-gather = f32[8,10,1,128]{3,2,1,0:T(1,128)S(1)} all-gather(f32[2,10,1,128]{3,2,1,0:T(1,128)S(1)} %maximum_add_fusion), channel_id=2, replica_groups=mesh['outer'=4,'dev'=8] {'outer'}, dimensions={0}, use_global_device_ids=true | all-gather | bytes 51200 | tf_op jit(solution)/shard_map/all_gather | solution.py:512
  118.0 3.5 %shard_map.102 = (f32[128,2560]{1,0:T(8,128)}, f32[128,1280]{1,0:T(8,128)S(1)}) custom-call(s32[1]{0:T(128)} %bitcast.pod_ref, f32[4,2,10,1,128]{4,3,2,1,0:T(1,128)S(1)} %bitcast.39, f32[2,5,64,512]{3,2,1,0:T(8,128)S(1)} %get-tuple-element.143.rows_ref, bf16[2,5,512,256]{3,2,1,0:T(8,128)(2,1)S(1)} %get-tuple-element.144.cols_ref, ...), custom_call_target="tpu_custom_call" | custom-call | flops 838860800 | bytes 1966080 | tf_op jit(solution)/shard_map/pallas_call | solution.py:229
  121.5 3.5 %shard_map.103 = (f32[128,2560]{1,0:T(8,128)}, f32[128,1280]{1,0:T(8,128)S(1)}) custom-call(s32[1]{0:T(128)} %bitcast.pod_ref, f32[4,2,10,1,128]{4,3,2,1,0:T(1,128)S(1)} %bitcast.40, f32[2,5,64,512]{3,2,1,0:T(8,128)S(1)} %get-tuple-element.150.rows_ref, bf16[2,5,512,256]{3,2,1,0:T(8,128)(2,1)S(1)} %get-tuple-element.151.cols_ref, ...), custom_call_target="tpu_custom_call", output_to_operand_aliasing={{0}: (7, {})} | custom-call | flops 838860800 | bytes 1966080 | tf_op jit(solution)/shard_map/pallas_call | solution.py:229
  (131 shorter events, 48.1 us)
Async XLA Ops:
  1.7 31.9 %collective-permute-start = (f32[64,1280]{1,0:T(8,128)S(1)}, f32[64,1280]{1,0:T(8,128)S(1)}, u32[]{:S(2)}, u32[]{:S(2)}) collective-permute-start(f32[64,1280]{1,0:T(8,128)S(1)} %get-tuple-element.84), channel_id=1, source_target_pairs={{0,1},{2,0},{4,2},{6,4},{7,6},{5,7},{3,5},{1,3},{8,9},{10,8},{12,1... | collective-permute-start | bytes 983048 | tf_op jit(solution)/shard_map/ppermute | solution.py:491
  4.7 21.5 %collective-permute-start.1 = (f32[64,1280]{1,0:T(8,128)S(1)}, f32[64,1280]{1,0:T(8,128)S(1)}, u32[]{:S(2)}, u32[]{:S(2)}) collective-permute-start(f32[64,1280]{1,0:T(8,128)S(1)} %get-tuple-element.85), channel_id=1, source_target_pairs={{0,2},{2,4},{4,6},{6,7},{7,5},{5,3},{3,1},{1,0},{8,10},{10,12},{12... | collective-permute-start | bytes 983048 | tf_op jit(solution)/shard_map/ppermute | solution.py:491
  5.9 30.4 %collective-permute-start.5 = (f32[64,1280]{1,0:T(8,128)S(1)}, f32[64,1280]{1,0:T(8,128)S(1)}, u32[]{:S(2)}, u32[]{:S(2)}) collective-permute-start(f32[64,1280]{1,0:T(8,128)S(1)} %get-tuple-element.87), channel_id=1, source_target_pairs={{0,2},{2,4},{4,6},{6,7},{7,5},{5,3},{3,1},{1,0},{8,10},{10,12},{12... | collective-permute-start | bytes 983048 | tf_op jit(solution)/shard_map/ppermute | solution.py:491
  9.2 11.8 %collective-permute-start.11 = (s32[10,1,128]{2,1,0:T(1,128)S(1)}, s32[10,1,128]{2,1,0:T(1,128)S(1)}, u32[]{:S(2)}, u32[]{:S(2)}) collective-permute-start(s32[10,1,128]{2,1,0:T(1,128)S(1)} %get-tuple-element.180), channel_id=1, source_target_pairs={{0,2},{2,4},{4,6},{6,7},{7,5},{5,3},{3,1},{1,0},{8,10},{10,12},{12... | collective-permute-start | bytes 15368 | tf_op jit(solution)/shard_map/ppermute | solution.py:444
  24.6 12.2 %collective-permute-start.4 = (f32[64,1280]{1,0:T(8,128)S(1)}, f32[64,1280]{1,0:T(8,128)S(1)}, u32[]{:S(2)}, u32[]{:S(2)}) collective-permute-start(f32[64,1280]{1,0:T(8,128)S(1)} %get-tuple-element.88), channel_id=1, source_target_pairs={{0,1},{2,0},{4,2},{6,4},{7,6},{5,7},{3,5},{1,3},{8,9},{10,8},{12,1... | collective-permute-start | bytes 983048 | tf_op jit(solution)/shard_map/ppermute | solution.py:491
  26.7 11.7 %collective-permute-start.3 = (f32[64,1280]{1,0:T(8,128)S(1)}, f32[64,1280]{1,0:T(8,128)S(1)}, u32[]{:S(2)}, u32[]{:S(2)}) collective-permute-start(f32[64,1280]{1,0:T(8,128)S(1)} %shard_map.89), channel_id=1, source_target_pairs={{0,2},{2,4},{4,6},{6,7},{7,5},{5,3},{3,1},{1,0},{8,10},{10,12},{12... | collective-permute-start | bytes 983048 | tf_op jit(solution)/shard_map/ppermute | solution.py:491
  36.3 13.9 %collective-permute-start.7 = (f32[64,1280]{1,0:T(8,128)S(1)}, f32[64,1280]{1,0:T(8,128)S(1)}, u32[]{:S(2)}, u32[]{:S(2)}) collective-permute-start(f32[64,1280]{1,0:T(8,128)S(1)} %shard_map.92), channel_id=1, source_target_pairs={{0,2},{2,4},{4,6},{6,7},{7,5},{5,3},{3,1},{1,0},{8,10},{10,12},{12... | collective-permute-start | bytes 983048 | tf_op jit(solution)/shard_map/ppermute | solution.py:491
  36.9 14.4 %collective-permute-start.6 = (f32[64,1280]{1,0:T(8,128)S(1)}, f32[64,1280]{1,0:T(8,128)S(1)}, u32[]{:S(2)}, u32[]{:S(2)}) collective-permute-start(f32[64,1280]{1,0:T(8,128)S(1)} %shard_map.93), channel_id=1, source_target_pairs={{0,1},{2,0},{4,2},{6,4},{7,6},{5,7},{3,5},{1,3},{8,9},{10,8},{12,1... | collective-permute-start | bytes 983048 | tf_op jit(solution)/shard_map/ppermute | solution.py:491
  45.2 13.1 %collective-permute-start.8 = (f32[64,1280]{1,0:T(8,128)S(1)}, f32[64,1280]{1,0:T(8,128)S(1)}, u32[]{:S(2)}, u32[]{:S(2)}) collective-permute-start(f32[64,1280]{1,0:T(8,128)S(1)} %convert_add_fusion.18), channel_id=1, source_target_pairs={{0,1},{2,0},{4,2},{6,4},{7,6},{5,7},{3,5},{1,3},{8,9},{10,8},{12,1... | collective-permute-start | bytes 983048 | tf_op jit(solution)/shard_map/ppermute | solution.py:491
  50.3 12.8 %collective-permute-start.15 = (f32[64,1280]{1,0:T(8,128)S(1)}, f32[64,1280]{1,0:T(8,128)S(1)}, u32[]{:S(2)}, u32[]{:S(2)}) collective-permute-start(f32[64,1280]{1,0:T(8,128)S(1)} %convert_add_fusion.17), channel_id=1, source_target_pairs={{0,2},{2,4},{4,6},{6,7},{7,5},{5,3},{3,1},{1,0},{8,10},{10,12},{12... | collective-permute-start | bytes 983048 | tf_op jit(solution)/shard_map/ppermute | solution.py:491
  51.3 14.0 %collective-permute-start.14 = (f32[64,1280]{1,0:T(8,128)S(1)}, f32[64,1280]{1,0:T(8,128)S(1)}, u32[]{:S(2)}, u32[]{:S(2)}) collective-permute-start(f32[64,1280]{1,0:T(8,128)S(1)} %convert_add_fusion.16), channel_id=1, source_target_pairs={{0,1},{2,0},{4,2},{6,4},{7,6},{5,7},{3,5},{1,3},{8,9},{10,8},{12,1... | collective-permute-start | bytes 983048 | tf_op jit(solution)/shard_map/ppermute | solution.py:491
  58.3 13.8 %collective-permute-start.21 = (f32[64,1280]{1,0:T(8,128)S(1)}, f32[64,1280]{1,0:T(8,128)S(1)}, u32[]{:S(2)}, u32[]{:S(2)}) collective-permute-start(f32[64,1280]{1,0:T(8,128)S(1)} %convert_add_fusion.14), channel_id=1, source_target_pairs={{0,1},{2,0},{4,2},{6,4},{7,6},{5,7},{3,5},{1,3},{8,9},{10,8},{12,1... | collective-permute-start | bytes 983048 | tf_op jit(solution)/shard_map/ppermute | solution.py:491
  65.4 11.9 %collective-permute-start.25 = (f32[64,1280]{1,0:T(8,128)S(1)}, f32[64,1280]{1,0:T(8,128)S(1)}, u32[]{:S(2)}, u32[]{:S(2)}) collective-permute-start(f32[64,1280]{1,0:T(8,128)S(1)} %convert_add_fusion.12), channel_id=1, source_target_pairs={{0,1},{2,0},{4,2},{6,4},{7,6},{5,7},{3,5},{1,3},{8,9},{10,8},{12,1... | collective-permute-start | bytes 983048 | tf_op jit(solution)/shard_map/ppermute | solution.py:491
  69.9 11.8 %collective-permute-start.18 = (f32[10,1,128]{2,1,0:T(1,128)S(1)}, f32[10,1,128]{2,1,0:T(1,128)S(1)}, u32[]{:S(2)}, u32[]{:S(2)}) collective-permute-start(f32[10,1,128]{2,1,0:T(1,128)S(1)} %get-tuple-element.182), channel_id=1, source_target_pairs={{0,4},{2,6},{4,7},{6,5},{7,3},{5,1},{3,0},{1,2},{8,12},{10,14},{12... | collective-permute-start | bytes 15368 | tf_op jit(solution)/shard_map/ppermute | solution.py:444
  70.5 12.0 %collective-permute-start.16 = (f32[10,1,128]{2,1,0:T(1,128)S(1)}, f32[10,1,128]{2,1,0:T(1,128)S(1)}, u32[]{:S(2)}, u32[]{:S(2)}) collective-permute-start(f32[10,1,128]{2,1,0:T(1,128)S(1)} %get-tuple-element.183), channel_id=1, source_target_pairs={{0,2},{2,4},{4,6},{6,7},{7,5},{5,3},{3,1},{1,0},{8,10},{10,12},{12... | collective-permute-start | bytes 15368 | tf_op jit(solution)/shard_map/ppermute | solution.py:444
  72.1 13.6 %collective-permute-start.17 = (f32[10,1,128]{2,1,0:T(1,128)S(1)}, f32[10,1,128]{2,1,0:T(1,128)S(1)}, u32[]{:S(2)}, u32[]{:S(2)}) collective-permute-start(f32[10,1,128]{2,1,0:T(1,128)S(1)} %get-tuple-element.184), channel_id=1, source_target_pairs={{0,1},{2,0},{4,2},{6,4},{7,6},{5,7},{3,5},{1,3},{8,9},{10,8},{12,1... | collective-permute-start | bytes 15368 | tf_op jit(solution)/shard_map/ppermute | solution.py:444
  77.3 13.4 %collective-permute-start.29 = (f32[64,1280]{1,0:T(8,128)S(1)}, f32[64,1280]{1,0:T(8,128)S(1)}, u32[]{:S(2)}, u32[]{:S(2)}) collective-permute-start(f32[64,1280]{1,0:T(8,128)S(1)} %convert_add_fusion.11.refs_0_), channel_id=1, source_target_pairs={{0,2},{2,4},{4,6},{6,7},{7,5},{5,3},{3,1},{1,0},{8,10},{10,12},{12... | collective-permute-start | bytes 983048 | tf_op jit(solution)/shard_map/ppermute | solution.py:491
  85.7 20.7 %collective-permute-start.32 = (f32[64,1280]{1,0:T(8,128)S(1)}, f32[64,1280]{1,0:T(8,128)S(1)}, u32[]{:S(2)}, u32[]{:S(2)}) collective-permute-start(f32[64,1280]{1,0:T(8,128)S(1)} %convert_add_fusion.8.refs_1_), channel_id=1, source_target_pairs={{0,1},{2,0},{4,2},{6,4},{7,6},{5,7},{3,5},{1,3},{8,9},{10,8},{12,1... | collective-permute-start | bytes 983048 | tf_op jit(solution)/shard_map/ppermute | solution.py:491
  85.7 18.5 %collective-permute-start.33 = (f32[64,1280]{1,0:T(8,128)S(1)}, f32[64,1280]{1,0:T(8,128)S(1)}, u32[]{:S(2)}, u32[]{:S(2)}) collective-permute-start(f32[64,1280]{1,0:T(8,128)S(1)} %convert_add_fusion.9.refs_0_), channel_id=1, source_target_pairs={{0,2},{2,4},{4,6},{6,7},{7,5},{5,3},{3,1},{1,0},{8,10},{10,12},{12... | collective-permute-start | bytes 983048 | tf_op jit(solution)/shard_map/ppermute | solution.py:491
  90.2 13.1 %collective-permute-start.28 = (f32[64,1280]{1,0:T(8,128)S(1)}, f32[64,1280]{1,0:T(8,128)S(1)}, u32[]{:S(2)}, u32[]{:S(2)}) collective-permute-start(f32[64,1280]{1,0:T(8,128)S(1)} %convert_add_fusion.10.refs_1_), channel_id=1, source_target_pairs={{0,1},{2,0},{4,2},{6,4},{7,6},{5,7},{3,5},{1,3},{8,9},{10,8},{12,1... | collective-permute-start | bytes 983048 | tf_op jit(solution)/shard_map/ppermute | solution.py:491
  90.8 16.5 %collective-permute-start.31 = (f32[64,1280]{1,0:T(8,128)S(1)}, f32[64,1280]{1,0:T(8,128)S(1)}, u32[]{:S(2)}, u32[]{:S(2)}) collective-permute-start(f32[64,1280]{1,0:T(8,128)S(1)} %convert_add_fusion.7), channel_id=1, source_target_pairs={{0,2},{2,4},{4,6},{6,7},{7,5},{5,3},{3,1},{1,0},{8,10},{10,12},{12... | collective-permute-start | bytes 983048 | tf_op jit(solution)/shard_map/ppermute | solution.py:491
  104.3 11.5 %collective-permute-start.35 = (f32[64,1280]{1,0:T(8,128)S(1)}, f32[64,1280]{1,0:T(8,128)S(1)}, u32[]{:S(2)}, u32[]{:S(2)}) collective-permute-start(f32[64,1280]{1,0:T(8,128)S(1)} %convert_add_fusion.5), channel_id=1, source_target_pairs={{0,2},{2,4},{4,6},{6,7},{7,5},{5,3},{3,1},{1,0},{8,10},{10,12},{12... | collective-permute-start | bytes 983048 | tf_op jit(solution)/shard_map/ppermute | solution.py:491
  107.3 17.6 %collective-permute-start.38 = (f32[64,1280]{1,0:T(8,128)S(1)}, f32[64,1280]{1,0:T(8,128)S(1)}, u32[]{:S(2)}, u32[]{:S(2)}) collective-permute-start(f32[64,1280]{1,0:T(8,128)S(1)} %convert_add_fusion.3), channel_id=1, source_target_pairs={{0,2},{2,4},{4,6},{6,7},{7,5},{5,3},{3,1},{1,0},{8,10},{10,12},{12... | collective-permute-start | bytes 983048 | tf_op jit(solution)/shard_map/ppermute | solution.py:491
  110.5 14.5 %collective-permute-start.39 = (f32[64,1280]{1,0:T(8,128)S(1)}, f32[64,1280]{1,0:T(8,128)S(1)}, u32[]{:S(2)}, u32[]{:S(2)}) collective-permute-start(f32[64,1280]{1,0:T(8,128)S(1)} %convert_add_fusion.2), channel_id=1, source_target_pairs={{0,1},{2,0},{4,2},{6,4},{7,6},{5,7},{3,5},{1,3},{8,9},{10,8},{12,1... | collective-permute-start | bytes 983048 | tf_op jit(solution)/shard_map/ppermute | solution.py:491
  (24 other events, 308.0 us)
